TPU v7x, 32 devices: a whole 2x2x4 slice. The times are simulated.
32 devices in a mesh: dp: 8 (over z, y), tensor: 4 (over x, core).
Axes of the slice: x: 2, y: 2, z: 4, core: 2. Of those that a mesh axis runs over, the one named last changes fastest.
Arguments:
- tokens: bfloat16 [16384, 768], P('dp'), may hold values from -6 to 6
- w_query: bfloat16 [768, 768], P(None, 'tensor'), may hold values from -0.21875 to 0.21875
- w_key: bfloat16 [768, 768], P(None, 'tensor'), may hold values from -0.21875 to 0.21875
- w_value: bfloat16 [768, 768], P(None, 'tensor'), may hold values from -0.21875 to 0.21875
- b_query: float32 [768], P('tensor'), may hold values from -4 to 4
- b_value: float32 [768], P('tensor'), may hold values from -3 to 3
- conv_taps: float32 [12, 33], P('tensor'), may hold values from -0.3 to 0.3
- w_out: bfloat16 [768, 768], P('tensor'), may hold values from -0.875 to 0.875
- b_out: float32 [768], replicated, may hold values from -3 to 3
- gain_one: float32 [768], replicated, may hold values from 0.5 to 1.5
- shift_one: float32 [768], replicated, may hold values from -3 to 3
- w_up: bfloat16 [768, 3072], P(None, 'tensor'), may hold values from -0.21875 to 0.21875
- b_up: float32 [3072], P('tensor'), may hold values from -3 to 3
- w_down: bfloat16 [3072, 768], P('tensor'), may hold values from -0.109375 to 0.109375
- b_down: float32 [768], replicated, may hold values from -3 to 3
- gain_two: float32 [768], replicated, may hold values from 0.5 to 1.5
- shift_two: float32 [768], replicated, may hold values from -3 to 3
- cotangent: bfloat16 [16384, 768], P(('dp', 'tensor')), may hold values from -6 to 6
- segment_ids: int32 [16384], P('dp'), may hold values from 0 to 7, as said below
- landmark_ids: int32 [16384], P('dp'), may hold values from 0 to 63, as said below
Outputs:
- layer_out: bfloat16 [16384, 768], P(('dp', 'tensor'))
- input_grad: float32 [16384, 768], P(('dp', 'tensor'))
- grad_w_query: float32 [768, 768], P(None, 'tensor')
- grad_w_key: float32 [768, 768], P(None, 'tensor')
- grad_w_value: float32 [768, 768], P(None, 'tensor')
- grad_b_query: float32 [768], P('tensor')
- grad_b_value: float32 [768], P('tensor')
- grad_conv: float32 [12, 33], P('tensor')
- grad_w_out: float32 [768, 768], P('tensor')
- grad_b_out: float32 [768], replicated
- grad_gain_one: float32 [768], replicated
- grad_shift_one: float32 [768], replicated
- grad_w_up: float32 [768, 3072], P(None, 'tensor')
- grad_b_up: float32 [3072], P('tensor')
- grad_w_down: float32 [3072, 768], P('tensor')
- grad_b_down: float32 [768], replicated
- grad_gain_two: float32 [768], replicated
- grad_shift_two: float32 [768], replicated
Inputs may be any that keep to these rules, and one draw needn't show every extreme that they name: `segment_ids`: within each sequence of 1024 tokens the ids never fall and take every value from 0 to 7; every document holds 64 tokens or more. `landmark_ids`: within each sequence every id from 0 to 63 occurs, and the tokens with id j form one run inside document j // 8.
All inputs are finite; a program needn't handle non-finite values.
Results may differ from a plain program's by a relative error of at most 0.015.
Values may be sent and summed in bfloat16 or wider, within the bound.
No kernel may reach another device: no remote copies, remote signals or barrier semaphores. Data moves between devices by JAX's collectives and lax.ppermute only.
A program may use at most 256 MiB of HBM per device.

v0:
```python
import jax
import jax.numpy as jnp
from jax import lax
from jax.sharding import PartitionSpec as P

HEAD_DIM = 64
LANDMARKS = 64
CONV_TAPS = 33
PINV_STEPS = 6
DOCS = 8
SEQ_LEN = 1024


HIGH = lax.Precision.HIGHEST
EPSILON = 1e-05


def softmax_masked(scores, allowed):
    masked = jnp.where(allowed, scores, -1e30)
    highest = jnp.max(masked, axis=-1, keepdims=True)
    expo = jnp.exp(masked - highest)
    return expo / jnp.sum(expo, axis=-1, keepdims=True)


def layer_norm(inputs, scaling, offsets):
    centered = inputs - jnp.mean(inputs, axis=-1, keepdims=True)
    variance = jnp.mean(centered * centered, axis=-1, keepdims=True)
    return centered * lax.rsqrt(variance + EPSILON) * scaling + offsets


def gelu_exact(inputs):
    return jax.nn.gelu(inputs, approximate=False)


def nystrom(queries, key_rows, values, conv_weights, segment, landmark):
    row_count = queries.shape[0]
    head_count = queries.shape[1]
    score_scale = queries.shape[2] ** (-0.5)
    one_hot = (landmark[None, :] == jnp.arange(LANDMARKS, dtype=jnp.int32)[:, None]).astype(
        queries.dtype
    )
    pooling = one_hot / jnp.sum(one_hot, axis=1, keepdims=True)
    land_doc = jnp.arange(LANDMARKS, dtype=jnp.int32) // (LANDMARKS // DOCS)
    near_mask = segment[:, None] == land_doc[None, :]
    mark_mask = land_doc[:, None] == land_doc[None, :]
    key_marks = jnp.einsum("jt,the->jhe", pooling, key_rows, precision=HIGH)
    query_marks = jnp.einsum("jt,the->jhe", pooling, queries, precision=HIGH)
    kernel_one = softmax_masked(
        jnp.einsum("the,jhe->htj", queries, key_marks, precision=HIGH) * score_scale,
        near_mask[None],
    )
    middle = softmax_masked(
        jnp.einsum("ihe,jhe->hij", query_marks, key_marks, precision=HIGH) * score_scale,
        mark_mask[None],
    )
    kernel_last = softmax_masked(
        jnp.einsum("jhe,the->hjt", query_marks, key_rows, precision=HIGH) * score_scale,
        near_mask.T[None],
    )
    column_most = jnp.max(jnp.sum(middle, axis=1), axis=1)
    row_most = jnp.max(jnp.sum(middle, axis=2), axis=1)
    inverse = jnp.swapaxes(middle, 1, 2) / (column_most * row_most)[:, None, None]
    identity = jnp.eye(LANDMARKS, dtype=middle.dtype)
    for sweep in range(PINV_STEPS):
        product = jnp.einsum("hij,hjk->hik", middle, inverse, precision=HIGH)
        inner_term = 7.0 * identity - product
        inner_term = 15.0 * identity - jnp.einsum(
            "hij,hjk->hik", product, inner_term, precision=HIGH
        )
        inner_term = 13.0 * identity - jnp.einsum(
            "hij,hjk->hik", product, inner_term, precision=HIGH
        )
        inverse = 0.25 * jnp.einsum("hij,hjk->hik", inverse, inner_term, precision=HIGH)
    context = jnp.einsum("hjt,the->hje", kernel_last, values, precision=HIGH)
    blended = jnp.einsum("hij,hje->hie", inverse, context, precision=HIGH)
    attended = jnp.einsum("htj,hje->the", kernel_one, blended, precision=HIGH)
    half_width = CONV_TAPS // 2
    padded = jnp.pad(values, ((half_width, half_width), (0, 0), (0, 0)))
    seg_pad = jnp.pad(segment, (half_width, half_width), constant_values=-1)
    for offset in range(CONV_TAPS):
        same_doc = (seg_pad[offset : offset + row_count] == segment).astype(values.dtype)
        attended = (
            attended
            + conv_weights[:, offset][None, :, None]
            * padded[offset : offset + row_count]
            * same_doc[:, None, None]
        )
    return attended.reshape(row_count, head_count * values.shape[2])


def contract_rows(left, right):
    return lax.dot_general(
        left, right, (((0,), (0,)), ((), ())), preferred_element_type=jnp.float32
    )


def contract_cols(left, right):
    return lax.dot_general(
        left, right, (((1,), (1,)), ((), ())), preferred_element_type=jnp.float32
    )


def per_device(
    tokens,
    w_query,
    w_key,
    w_value,
    b_query,
    b_value,
    conv_taps,
    w_out,
    b_out,
    gain_one,
    shift_one,
    w_up,
    b_up,
    w_down,
    b_down,
    gain_two,
    shift_two,
    cotangent,
    segment_ids,
    landmark_ids,
):
    share_rows = tokens.shape[0] // lax.axis_size("tensor")
    first_row = lax.axis_index("tensor") * share_rows
    local_dim = w_query.shape[1]
    head_count = local_dim // HEAD_DIM
    seq_count = tokens.shape[0] // SEQ_LEN
    shaped = (seq_count, SEQ_LEN, head_count, HEAD_DIM)
    segments = segment_ids.reshape(seq_count, SEQ_LEN)
    marks = landmark_ids.reshape(seq_count, SEQ_LEN)
    queries = (jnp.dot(tokens, w_query, preferred_element_type=jnp.float32) + b_query).astype(
        jnp.bfloat16
    )
    key_rows = jnp.dot(tokens, w_key, preferred_element_type=jnp.float32).astype(jnp.bfloat16)
    values = (jnp.dot(tokens, w_value, preferred_element_type=jnp.float32) + b_value).astype(
        jnp.bfloat16
    )
    float_query = queries.astype(jnp.float32).reshape(shaped)
    float_key = key_rows.astype(jnp.float32).reshape(shaped)
    float_value = values.astype(jnp.float32).reshape(shaped)

    def attend(query_all, key_all, value_all, weights):
        return jax.vmap(nystrom, in_axes=(0, 0, 0, None, 0, 0))(
            query_all, key_all, value_all, weights, segments, marks
        )

    attended_f, attend_back = jax.vjp(attend, float_query, float_key, float_value, conv_taps)
    attended = attended_f.reshape(tokens.shape[0], local_dim).astype(jnp.bfloat16)
    summed = lax.psum_scatter(
        jnp.dot(attended, w_out, preferred_element_type=jnp.float32),
        "tensor",
        scatter_dimension=0,
        tiled=True,
    )
    own_tokens = lax.dynamic_slice_in_dim(tokens, first_row, share_rows, 0).astype(jnp.float32)
    normed, norm_back_one = jax.vjp(layer_norm, own_tokens + summed + b_out, gain_one, shift_one)
    normed_low = lax.all_gather(normed.astype(jnp.bfloat16), "tensor", axis=0, tiled=True)
    hidden = jnp.dot(normed_low, w_up, preferred_element_type=jnp.float32) + b_up
    activated_f, gelu_back = jax.vjp(gelu_exact, hidden)
    activated = activated_f.astype(jnp.bfloat16)
    branch = lax.psum_scatter(
        jnp.dot(activated, w_down, preferred_element_type=jnp.float32),
        "tensor",
        scatter_dimension=0,
        tiled=True,
    )
    output, norm_back_two = jax.vjp(layer_norm, normed + branch + b_down, gain_two, shift_two)
    grad_pre_out, grad_gain_two, grad_shift_two = norm_back_two(cotangent.astype(jnp.float32))
    grad_b_down = jnp.sum(grad_pre_out, axis=0)
    grad_branch = lax.all_gather(grad_pre_out.astype(jnp.bfloat16), "tensor", axis=0, tiled=True)
    grad_w_down = contract_rows(activated, grad_branch)
    grad_act = contract_cols(grad_branch, w_down)
    grad_hidden = gelu_back(grad_act)[0].astype(jnp.bfloat16)
    grad_w_up = contract_rows(normed_low, grad_hidden)
    grad_b_up = jnp.sum(grad_hidden, axis=0, dtype=jnp.float32)
    back_normed = lax.psum_scatter(
        contract_cols(grad_hidden, w_up).astype(jnp.bfloat16),
        "tensor",
        scatter_dimension=0,
        tiled=True,
    ).astype(jnp.float32)
    back_normed = lax.optimization_barrier(back_normed.astype(jnp.bfloat16)).astype(jnp.float32)
    grad_pre_norm, grad_gain_one, grad_shift_one = norm_back_one(grad_pre_out + back_normed)
    grad_b_out = jnp.sum(grad_pre_norm, axis=0)
    grad_summed = lax.all_gather(grad_pre_norm.astype(jnp.bfloat16), "tensor", axis=0, tiled=True)
    grad_w_out = contract_rows(attended, grad_summed)
    grad_attended = contract_cols(grad_summed, w_out).reshape(seq_count, SEQ_LEN, local_dim)
    grad_q_f, grad_k_f, grad_v_f, grad_conv = attend_back(grad_attended)
    grad_queries = grad_q_f.reshape(tokens.shape[0], local_dim).astype(jnp.bfloat16)
    grad_keys = grad_k_f.reshape(tokens.shape[0], local_dim).astype(jnp.bfloat16)
    grad_values = grad_v_f.reshape(tokens.shape[0], local_dim).astype(jnp.bfloat16)
    grad_w_query = contract_rows(tokens, grad_queries)
    grad_w_key = contract_rows(tokens, grad_keys)
    grad_w_value = contract_rows(tokens, grad_values)
    grad_b_query = jnp.sum(grad_queries, axis=0, dtype=jnp.float32)
    grad_b_value = jnp.sum(grad_values, axis=0, dtype=jnp.float32)
    total = contract_cols(grad_queries, w_query)
    total = total + contract_cols(grad_keys, w_key)
    input_grad = grad_pre_norm + lax.psum_scatter(
        (total + contract_cols(grad_values, w_value)).astype(jnp.bfloat16),
        "tensor",
        scatter_dimension=0,
        tiled=True,
    ).astype(jnp.float32)
    (
        grad_w_query,
        grad_w_key,
        grad_w_value,
        grad_b_query,
        grad_b_value,
        grad_conv,
        grad_w_out,
        grad_w_up,
        grad_w_down,
        grad_b_up,
    ) = lax.psum(
        (
            grad_w_query,
            grad_w_key,
            grad_w_value,
            grad_b_query,
            grad_b_value,
            grad_conv,
            grad_w_out,
            grad_w_up,
            grad_w_down,
            grad_b_up,
        ),
        "dp",
    )
    grad_gain_one, grad_shift_one, grad_b_out, grad_gain_two, grad_shift_two, grad_b_down = (
        lax.psum(
            (grad_gain_one, grad_shift_one, grad_b_out, grad_gain_two, grad_shift_two, grad_b_down),
            ("dp", "tensor"),
        )
    )
    return (
        output.astype(jnp.bfloat16),
        input_grad,
        grad_w_query,
        grad_w_key,
        grad_w_value,
        grad_b_query,
        grad_b_value,
        grad_conv,
        grad_w_out,
        grad_b_out,
        grad_gain_one,
        grad_shift_one,
        grad_w_up,
        grad_b_up,
        grad_w_down,
        grad_b_down,
        grad_gain_two,
        grad_shift_two,
    )


def solution(mesh):
    return jax.shard_map(
        per_device,
        mesh=mesh,
        in_specs=(
            P("dp", None),
            P(None, "tensor"),
            P(None, "tensor"),
            P(None, "tensor"),
            P("tensor"),
            P("tensor"),
            P("tensor", None),
            P("tensor", None),
            P(),
            P(),
            P(),
            P(None, "tensor"),
            P("tensor"),
            P("tensor", None),
            P(),
            P(),
            P(),
            P(("dp", "tensor"), None),
            P("dp"),
            P("dp"),
        ),
        out_specs=(
            P(("dp", "tensor"), None),
            P(("dp", "tensor"), None),
            P(None, "tensor"),
            P(None, "tensor"),
            P(None, "tensor"),
            P("tensor"),
            P("tensor"),
            P("tensor", None),
            P("tensor", None),
            P(),
            P(),
            P(),
            P(None, "tensor"),
            P("tensor"),
            P("tensor", None),
            P(),
            P(),
            P(),
        ),
        check_vma=False,
    )
```

profile of v0, /device:TPU:0, one launch (start us, length us, event | category | flops | bytes accessed | tf_op | source)
XLA Modules:
  0.0 814.5 jit_solution(1764736523739853846)
XLA Ops:
  7.3 2.2 slice_reduce_fusion.31
  9.5 2.4 slice_reduce_fusion.32
  17.3 3.2 fusion.7
  22.0 2.5 reshape.559
  24.8 3.1 fusion.6
  28.8 4.2 convolution_convert_fusion.1
  33.1 2.8 reshape.557
  61.6 15.7 %add_convert_fusion.3 = bf16[2,1024,3,64]{1,3,2,0:T(8,128)(2,1)S(1)} fusion(f32[2,1024,3,64]{1,3,2,0:T(8,128)S(1)} %copy.171, f32[2,3,64,64]{3,2,1,0:T(8,128)S(1)} %fusion.182, f32[2,1024]{1,0:T(2,128)S(1)} %copy-done.179, f32[3]{0:T(128)} %get-tuple-element.144, f32[2,1024]{1,0:T(2,128)S(1)} %copy-done.143, f32[3]{0:T(128)} %get-tuple-element.145, ...), kind=kOutput, calls=%fused_computation.126 | convolution fusion | flops 341704704 | bytes 4342156 | tf_op jit(solution)/shard_map/jvp(vmap(htj,hje->the))/dot_general | solution.py:76
  78.4 3.7 fusion.183
  82.2 61.1 %reduce-scatter.5.cloned.1.call-done = f32[512,768]{1,0:T(8,128)} async-done(((f32[2048,768]{1,0:T(8,128)}), f32[512,768]{1,0:T(8,128)}) %reduce-scatter.5.cloned.1.call-update) | async-done | bytes 1572880 | tf_op jit(solution)/shard_map/reduce_scatter | solution.py:151
  147.2 28.6 %all-gather.4.cloned.1.call-done = bf16[2048,768]{1,0:T(8,128)(2,1)} async-done(((bf16[512,768]{1,0:T(8,128)(2,1)}), bf16[2048,768]{1,0:T(8,128)(2,1)}) %all-gather.4.cloned.1.call-update) | async-done | bytes 3145744 | tf_op jit(solution)/shard_map/all_gather | solution.py:159
  175.9 18.8 %multiply_convert_fusion = (bf16[2048,768]{1,0:T(8,128)(2,1)S(1)}, f32[2048,768]{1,0:T(8,128)}, f32[2048,768]{1,0:T(8,128)}) fusion(f32[768]{0:T(1024)S(1)} %copy-done.314, bf16[2048,768]{1,0:T(8,128)(2,1)} %all-gather.4.cloned.1.call-done, bf16[768,768]{1,0:T(8,128)(2,1)S(1)} %copy-done), kind=kOutput, calls=%fused_computation.5 | convolution fusion | flops 2519728128 | bytes 20057088 | tf_op jit(solution)/shard_map/dot_general | solution.py:160
  196.3 4.5 fusion.184
  200.9 58.5 %reduce-scatter.7.cloned.1.call-done = f32[512,768]{1,0:T(8,128)} async-done(((f32[2048,768]{1,0:T(8,128)}), f32[512,768]{1,0:T(8,128)}) %reduce-scatter.7.cloned.1.call-update) | async-done | bytes 1572880 | tf_op jit(solution)/shard_map/reduce_scatter | solution.py:163
  263.7 2.1 fusion.171
  265.8 2.4 add_convert_fusion.5
  268.3 28.7 %all-gather.6.cloned.1.call-done = bf16[2048,768]{1,0:T(8,128)(2,1)} async-done(((bf16[512,768]{1,0:T(8,128)(2,1)}), bf16[2048,768]{1,0:T(8,128)(2,1)}) %all-gather.6.cloned.1.call-update) | async-done | bytes 3145744 | tf_op jit(solution)/shard_map/all_gather | solution.py:172
  297.0 11.1 %convert_reduce_fusion = (f32[768]{0:T(1024)}, bf16[2048,768]{1,0:T(8,128)(2,1)S(1)}) fusion(f32[2048,768]{1,0:T(8,128)} %get-tuple-element.189, f32[2048,768]{1,0:T(8,128)} %get-tuple-element.276, f32[768]{0:T(1024)S(1)} %copy-done.314, bf16[2048,768]{1,0:T(8,128)(2,1)} %all-gather.6.cloned.1.call-done, bf16[768,768]{1,0:T(8,128)(2,1)} %param.33), kind=kOutput, calls=%fused_computation.2 | convolution fusion | flops 2442657024 | bytes 20060160 | tf_op jit(solution)/shard_map/dot_general | solution.py:98
  309.8 4.0 convolution_convert_fusion
  313.8 38.1 %reduce-scatter.9.cloned.1.call-done = bf16[512,768]{1,0:T(8,128)(2,1)} async-done(((bf16[2048,768]{1,0:T(8,128)(2,1)}), bf16[512,768]{1,0:T(8,128)(2,1)}) %reduce-scatter.9.cloned.1.call-update) | async-done | bytes 786448 | tf_op jit(solution)/shard_map/reduce_scatter | solution.py:178
  351.9 3.2 multiply_reduce_fusion
  355.1 3.3 fusion.170
  358.5 3.2 add_reduce_fusion
  365.0 25.4 %all-gather.8.cloned.1.call-done = bf16[2048,768]{1,0:T(8,128)(2,1)} async-done(((bf16[512,768]{1,0:T(8,128)(2,1)}), bf16[2048,768]{1,0:T(8,128)(2,1)}) %all-gather.8.cloned.1.call-update) | async-done | bytes 3145744 | tf_op jit(solution)/shard_map/all_gather | solution.py:187
  390.4 3.7 multiply_reduce_fusion.17
  395.5 3.5 fusion.41
  419.5 6.6 multiply_reduce_fusion.30
  426.2 5.1 multiply_multiply_fusion.17
  431.6 6.3 multiply_multiply_fusion.36
  438.1 5.6 multiply_multiply_fusion.26
  456.3 2.5 fusion.101
  458.9 2.6 convert_reduce_fusion.5
  462.4 3.4 convert_reduce_fusion.3
  472.7 2.2 fusion.14
  476.0 3.7 fusion.200
  479.8 3.7 fusion.199
  483.5 20.5 %pad_add_fusion = f32[2,1056,3,64]{1,3,2,0:T(8,128)} fusion(f32[2,1024,3,64]{1,3,2,0:T(8,128)} %get-tuple-element.229, f32[2,1024,3,64]{1,3,2,0:T(8,128)} %get-tuple-element.228, f32[2,1024,3,64]{1,3,2,0:T(8,128)} %get-tuple-element.227, f32[2,1024,3,64]{1,3,2,0:T(8,128)} %get-tuple-element.226, f32[2,1024,3,64]{1,3,2,0:T(8,128)} %get-tuple-element.225, ...), kind=kLoop, calls=%fused_computation.32 | loop fusion | flops 10543104 | bytes 44089344 | tf_op jit(solution)/shard_map/transpose(jvp(vmap()))/add_any | solution.py:85
  504.1 7.1 convert_reduce_fusion.2
  513.2 2.7 add_convert_fusion
  516.0 7.1 fusion.203
  523.1 4.2 fusion.202
  535.2 40.6 %all-reduce.68 = (f32[768]{0:T(1024)}, f32[768]{0:T(1024)}, f32[768]{0:T(1024)}, f32[768]{0:T(1024)}, f32[768]{0:T(1024)}, /*index=5*/f32[768]{0:T(1024)}) all-reduce(f32[768]{0:T(1024)S(1)} %copy-done.242, f32[768]{0:T(1024)S(1)} %copy-done.252, f32[768]{0:T(1024)S(1)} %copy-done.253, ...), channel_id=1, replica_groups=mesh['dp'=8,'tensor'=4] {'dp','tensor'}, use_global_device_ids=true, to_apply=%region_79.80 | all-reduce | flops 4608 | bytes 36864 | tf_op jit(solution)/shard_map/psum | solution.py:234
  576.3 4.0 multiply_reduce_fusion.31
  580.5 4.0 multiply_reduce_fusion.32
  584.7 4.0 multiply_reduce_fusion.33
  588.8 39.8 %all-reduce.69 = (f32[192]{0:T(256)}, f32[192]{0:T(256)}, f32[3,33]{0,1:T(8,128)S(1)}, f32[768]{0:T(1024)}) all-reduce(f32[192]{0:T(256)S(1)} %reduce_sum.660, f32[192]{0:T(256)S(1)} %reduce_sum.665, f32[3,33]{0,1:T(8,128)S(1)} %pad_add_fusion.7, f32[768]{0:T(1024)S(1)} %copy-done.268), channel_id=1, replica_groups=mesh['dp'=8,'tensor'=4] {'dp'}, use_global_device_ids=true, to_apply=%region_39.40 | all-reduce | flops 1251 | bytes 10008 | tf_op jit(solution)/shard_map/psum | solution.py:218
  629.3 3.1 convert_add_fusion
  632.4 166.7 %all-reduce.73.cloned.1.call-done = (f32[768,192]{0,1:T(8,128)}, f32[768,192]{0,1:T(8,128)}, f32[768,192]{0,1:T(8,128)}, f32[192,768]{1,0:T(8,128)}, f32[768,768]{1,0:T(8,128)}, /*index=5*/f32[768,768]{1,0:T(8,128)}) async-done(((f32[768,192]{0,1:T(8,128)}, f32[768,192]{0,1:T(8,128)}, f32[768,192]{0,1:T(8,128)}, f32[192,768]{1,0:T(8,128)}, f32[768,768]{1,0:T(8,128)}, /*index=5*/f32[768,768]{1,0:T(8,128)}), ...) | async-done | bytes 7077904 | tf_op jit(solution)/shard_map/psum | solution.py:218
  (828 shorter events, 109.6 us)
Async XLA Ops:
  7.2 168.7 %copy-start = (bf16[768,768]{1,0:T(8,128)(2,1)S(1)}, bf16[768,768]{1,0:T(8,128)(2,1)}, u32[]{:S(2)}) copy-start(bf16[768,768]{1,0:T(8,128)(2,1)} %param.31) | copy-start | bytes 3538948
  7.2 136.1 %reduce-scatter.5.cloned.1.call-start = ((), (), s32[]{:S(2)}) async-start(), calls=%async_computation.4 | async-start | bytes 7864320 | tf_op jit(solution)/shard_map/reduce_scatter | solution.py:151
  11.9 37.6 %copy-start.88 = (f32[64,64]{1,0:T(8,128)}, f32[64,64]{1,0:T(8,128)S(1)}, u32[]{:S(2)}) copy-start(f32[64,64]{1,0:T(8,128)S(1)} %fusion.149) | copy-start | bytes 49156
  11.9 37.3 %copy-start.36 = (f32[64,64]{1,0:T(8,128)}, f32[64,64]{1,0:T(8,128)S(1)}, u32[]{:S(2)}) copy-start(f32[64,64]{1,0:T(8,128)S(1)} %get-tuple-element.291) | copy-start | bytes 49156
  11.9 37.3 %copy-start.90 = (f32[64,64]{1,0:T(8,128)}, f32[64,64]{1,0:T(8,128)S(1)}, u32[]{:S(2)}) copy-start(f32[64,64]{1,0:T(8,128)S(1)} %get-tuple-element.292) | copy-start | bytes 49156
  24.5 12.5 %copy-start.234 = (s32[2,1024]{1,0:T(2,128)}, s32[2,1024]{1,0:T(2,128)S(1)}, u32[]{:S(2)}) copy-start(s32[2,1024]{1,0:T(2,128)S(1)} %eq.252) | copy-start | bytes 24580
  24.7 12.3 %copy-start.307 = (f32[2,64]{1,0:T(2,128)}, f32[2,64]{1,0:T(2,128)S(1)}, u32[]{:S(2)}) copy-start(f32[2,64]{1,0:T(2,128)S(1)} %convert_reduce_fusion.6) | copy-start | bytes 1540
  24.8 18.1 %copy-start.257 = (pred[64,64]{1,0:T(8,128)(4,1)}, pred[64,64]{1,0:T(8,128)(4,1)S(1)}, u32[]{:S(2)}) copy-start(pred[64,64]{1,0:T(8,128)(4,1)S(1)} %copy.157) | copy-start | bytes 12292
  28.8 7.0 copy-start.97
  60.8 16.5 %copy-start.123 = (f32[2,3,64,64]{3,2,1,0:T(8,128)}, f32[2,3,64,64]{3,2,1,0:T(8,128)S(1)}, u32[]{:S(2)}) copy-start(f32[2,3,64,64]{3,2,1,0:T(8,128)S(1)} %fusion.182) | copy-start | bytes 294916
  61.1 303.3 %copy-start.116 = (f32[2,3,1024]{2,1,0:T(4,128)}, f32[2,3,1024]{2,1,0:T(4,128)S(1)}, u32[]{:S(2)}) copy-start(f32[2,3,1024]{2,1,0:T(4,128)S(1)} %fusion.65) | copy-start | bytes 73732
  82.1 61.2 %copy-start.259 = (f32[768]{0:T(1024)S(1)}, f32[768]{0:T(1024)}, u32[]{:S(2)}) copy-start(f32[768]{0:T(1024)} %param.28) | copy-start | bytes 9220
  82.1 93.7 %all-gather.4.cloned.1.call-start = ((), (), s32[]{:S(2)}) async-start(), calls=%async_computation.5 | async-start | bytes 3932160 | tf_op jit(solution)/shard_map/all_gather | solution.py:159
  145.9 29.9 %copy-start.314 = (f32[768]{0:T(1024)S(1)}, f32[768]{0:T(1024)}, u32[]{:S(2)}) copy-start(f32[768]{0:T(1024)} %param.32) | copy-start | bytes 9220
  147.1 112.2 %reduce-scatter.7.cloned.1.call-start = ((), (), s32[]{:S(2)}) async-start(), calls=%async_computation.6 | async-start | bytes 7864320 | tf_op jit(solution)/shard_map/reduce_scatter | solution.py:163
  175.9 20.5 %copy-start.313 = (bf16[768,768]{1,0:T(8,128)(2,1)S(1)}, bf16[768,768]{1,0:T(8,128)(2,1)}, u32[]{:S(2)}) copy-start(bf16[768,768]{1,0:T(8,128)(2,1)} %param.33) | copy-start | bytes 3538948
  200.8 58.5 %copy-start.269 = (f32[768]{0:T(1024)S(1)}, f32[768]{0:T(1024)}, u32[]{:S(2)}) copy-start(f32[768]{0:T(1024)} %param.34) | copy-start | bytes 9220
  200.8 96.2 %all-gather.6.cloned.1.call-start = ((), (), s32[]{:S(2)}) async-start(), calls=%async_computation.7 | async-start | bytes 3932160 | tf_op jit(solution)/shard_map/all_gather | solution.py:172
  268.3 83.6 %reduce-scatter.9.cloned.1.call-start = ((), (), s32[]{:S(2)}) async-start(), calls=%async_computation.8 | async-start | bytes 3932160 | tf_op jit(solution)/shard_map/reduce_scatter | solution.py:178
  313.8 76.6 %all-gather.8.cloned.1.call-start = ((), (), s32[]{:S(2)}) async-start(), calls=%async_computation.9 | async-start | bytes 3932160 | tf_op jit(solution)/shard_map/all_gather | solution.py:187
  358.5 31.9 %copy-start.11 = (bf16[2048,192]{0,1:T(8,128)(2,1)S(1)}, bf16[2048,192]{0,1:T(8,128)(2,1)}, u32[]{:S(2)}) copy-start(bf16[2048,192]{0,1:T(8,128)(2,1)} %copy-done.10) | copy-start | bytes 2359300
  358.5 31.9 %copy-start.93 = (bf16[192,768]{1,0:T(8,128)(2,1)S(1)}, bf16[192,768]{1,0:T(8,128)(2,1)}, u32[]{:S(2)}) copy-start(bf16[192,768]{1,0:T(8,128)(2,1)} %param.27) | copy-start | bytes 884740
  361.7 267.6 %reduce-scatter.11.cloned.1.call-start = ((), (), s32[]{:S(2)}) async-start(), calls=%async_computation.10 | async-start | bytes 3932160 | tf_op jit(solution)/shard_map/reduce_scatter | solution.py:201
  399.9 47.9 %copy-start.106 = (f32[2,3,64,64]{3,2,1,0:T(8,128)}, f32[2,3,64,64]{3,2,1,0:T(8,128)S(1)}, u32[]{:S(2)}) copy-start(f32[2,3,64,64]{3,2,1,0:T(8,128)S(1)} %fusion.185) | copy-start | bytes 294916
  419.3 6.7 copy-start.183
  471.2 8.6 %copy-start.22 = (bf16[24,8,2,1024]{3,1,2,0:T(8,128)(2,1)}, bf16[24,8,2,1024]{3,1,2,0:T(8,128)(2,1)S(1)}, u32[]{:S(2)}) copy-start(bf16[24,8,2,1024]{3,1,2,0:T(8,128)(2,1)S(1)} %copy.273) | copy-start | bytes 2359300
  483.5 20.5 %copy-start.8 = (f32[2,3,64,1024]{3,2,1,0:T(8,128)S(1)}, f32[2,3,64,1024]{3,2,1,0:T(8,128)}, u32[]{:S(2)}) copy-start(f32[2,3,64,1024]{3,2,1,0:T(8,128)} %copy-done.6) | copy-start | bytes 4718596
  483.5 20.6 %copy-start.107 = (f32[2,3,64,64]{3,2,1,0:T(8,128)S(1)}, f32[2,3,64,64]{3,2,1,0:T(8,128)}, u32[]{:S(2)}) copy-start(f32[2,3,64,64]{3,2,1,0:T(8,128)} %copy-done.106) | copy-start | bytes 294916
  483.5 20.6 %copy-start.208 = (f32[2,3,64]{2,1,0:T(4,128)S(1)}, f32[2,3,64]{2,1,0:T(4,128)}, u32[]{:S(2)}) copy-start(f32[2,3,64]{2,1,0:T(4,128)} %copy-done.206) | copy-start | bytes 4612
  483.5 20.6 %copy-start.212 = (f32[2,3,64]{2,1,0:T(4,128)S(1)}, f32[2,3,64]{2,1,0:T(4,128)}, u32[]{:S(2)}) copy-start(f32[2,3,64]{2,1,0:T(4,128)} %copy-done.209) | copy-start | bytes 4612
  504.0 9.1 %slice-start = ((s8[6291456]{0:T(1024)(128)(4,1)}), s8[4194304]{0:T(1024)(128)(4,1)S(1)}, s32[]{:S(2)}) async-start(s8[6291456]{0:T(1024)(128)(4,1)} %bitcast.353), calls=%async_computation.12 | async-start | bytes 8388608
  504.1 9.1 %slice-start.1 = ((s8[6291456]{0:T(1024)(128)(4,1)}), s8[2097152]{0:T(1024)(128)(4,1)S(1)}, s32[]{:S(2)}) async-start(s8[6291456]{0:T(1024)(128)(4,1)} %bitcast.353), calls=%async_computation.13 | async-start | bytes 4194304
  504.1 9.1 %copy-start.4 = (f32[2048,768]{1,0:T(8,128)S(1)}, f32[2048,768]{1,0:T(8,128)}, u32[]{:S(2)}) copy-start(f32[2048,768]{1,0:T(8,128)} %fusion.199) | copy-start | bytes 18874372
  515.9 283.1 %all-reduce.73.cloned.1.call-start = ((), (), s32[]{:S(2)}) async-start(), calls=%async_computation.11 | async-start | bytes 14155776 | tf_op jit(solution)/shard_map/psum | solution.py:218
  516.0 7.1 copy-start.312
  516.0 7.1 copy-start.318
  534.5 41.3 %copy-start.261 = (f32[192]{0:T(256)S(1)}, f32[192]{0:T(256)}, u32[]{:S(2)}) copy-start(f32[192]{0:T(256)} %get-tuple-element.287) | copy-start | bytes 2308
  534.5 41.4 %copy-start.255 = (f32[3,64]{1,0:T(4,128)S(1)}, f32[3,64]{1,0:T(4,128)}, u32[]{:S(2)}) copy-start(f32[3,64]{1,0:T(4,128)} %get-tuple-element.283) | copy-start | bytes 2308
  534.5 41.7 %copy-start.148 = (f32[2,1024]{1,0:T(2,128)S(1)}, f32[2,1024]{1,0:T(2,128)}, u32[]{:S(2)}) copy-start(f32[2,1024]{1,0:T(2,128)} %get-tuple-element.244) | copy-start | bytes 24580
  534.5 41.7 %copy-start.151 = (f32[2,1024]{1,0:T(2,128)S(1)}, f32[2,1024]{1,0:T(2,128)}, u32[]{:S(2)}) copy-start(f32[2,1024]{1,0:T(2,128)} %get-tuple-element.245) | copy-start | bytes 24580
  534.5 41.7 %copy-start.154 = (f32[2,1024]{1,0:T(2,128)S(1)}, f32[2,1024]{1,0:T(2,128)}, u32[]{:S(2)}) copy-start(f32[2,1024]{1,0:T(2,128)} %get-tuple-element.246) | copy-start | bytes 24580
  534.5 41.7 %copy-start.157 = (f32[2,1024]{1,0:T(2,128)S(1)}, f32[2,1024]{1,0:T(2,128)}, u32[]{:S(2)}) copy-start(f32[2,1024]{1,0:T(2,128)} %get-tuple-element.247) | copy-start | bytes 24580
  534.5 41.7 %copy-start.160 = (f32[2,1024]{1,0:T(2,128)S(1)}, f32[2,1024]{1,0:T(2,128)}, u32[]{:S(2)}) copy-start(f32[2,1024]{1,0:T(2,128)} %get-tuple-element.248) | copy-start | bytes 24580
  534.5 41.7 %copy-start.163 = (f32[2,1024]{1,0:T(2,128)S(1)}, f32[2,1024]{1,0:T(2,128)}, u32[]{:S(2)}) copy-start(f32[2,1024]{1,0:T(2,128)} %get-tuple-element.249) | copy-start | bytes 24580
  534.6 41.7 %copy-start.166 = (f32[2,1024]{1,0:T(2,128)S(1)}, f32[2,1024]{1,0:T(2,128)}, u32[]{:S(2)}) copy-start(f32[2,1024]{1,0:T(2,128)} %get-tuple-element.236) | copy-start | bytes 24580
  534.6 41.7 %copy-start.169 = (f32[2,1024]{1,0:T(2,128)S(1)}, f32[2,1024]{1,0:T(2,128)}, u32[]{:S(2)}) copy-start(f32[2,1024]{1,0:T(2,128)} %get-tuple-element.241) | copy-start | bytes 24580
  534.6 41.7 %copy-start.172 = (f32[2,1024]{1,0:T(2,128)S(1)}, f32[2,1024]{1,0:T(2,128)}, u32[]{:S(2)}) copy-start(f32[2,1024]{1,0:T(2,128)} %get-tuple-element.242) | copy-start | bytes 24580
  584.7 44.7 %copy-start.237 = (f32[512]{0:T(512)S(1)}, f32[512]{0:T(512)}, u32[]{:S(2)}) copy-start(f32[512]{0:T(512)} %copy-done.236) | copy-start | bytes 6148
  (281 other events, 789.0 us)
Sparse Core Ops, SparseCore 0:
  82.3 61.0 reduce-scatter.4
  147.3 28.5 all-gather.3
  201.0 58.3 reduce-scatter.6
  268.4 28.5 all-gather.5
  313.9 37.9 reduce-scatter.8
  361.8 28.5 all-gather.7
  516.1 38.6 reduce-scatter.10
  561.0 238.0 all-reduce.72
where the time goes:
time: 822 us; the launch traced here: 815 us
  waiting for transfers between devices  407 us (50%)
  matrix products  169 us (21%)
  other arithmetic  92.7 us (11%)
  blocking collectives  80.5 us (10%)
  local copies, waits for them, and re-layouts  45.9 us (6%)
  between operations  19.3 us (2%)
    psum x1, waiting for transfers between devices, per_device(): lax.psum((grad_w_query, grad_w_key, grad_w_value, grad_b_query, grad_b_va...  167 us
    reduce_scatter x1, waiting for transfers between devices, per_device(): lax.psum_scatter(jnp.dot(attended, w_out, preferred_element_type=jnp.floa...  61.1 us
    reduce_scatter x1, waiting for transfers between devices, per_device(): lax.psum_scatter(jnp.dot(activated, w_down, preferred_element_type=jnp.fl...  58.5 us
    psum x1, blocking collectives, per_device(): lax.psum((grad_gain_one, grad_shift_one, grad_b_out, grad_gain_two, grad_...  40.6 us
    psum x1, blocking collectives, per_device(): lax.psum((grad_w_query, grad_w_key, grad_w_value, grad_b_query, grad_b_va...  39.8 us
    reduce_scatter x1, waiting for transfers between devices, per_device(): lax.psum_scatter(contract_cols(grad_hidden, w_up).astype(jnp.bfloat16), '...  38.1 us
    dot_general x6, matrix products, contract_cols(): lax.dot_general(left, right, (((1,), (1,)), ((), ())), preferred_element_...  29 us
    all_gather x1, waiting for transfers between devices, per_device(): lax.all_gather(grad_pre_out.astype(jnp.bfloat16), 'tensor', axis=0, tiled...  28.7 us
  transfers between devices with their start and end apart: 8, of which 7 were waited for; matrix products, arithmetic and copies ran while one was open for 5% of the time, Pallas kernels for 0%

commit v1 on v0

v1 whole, which is shorter than its diff:
```python
import jax
import jax.numpy as jnp
from jax import lax
from jax.experimental import pallas as pl
from jax.experimental.pallas import tpu as pltpu
from jax.sharding import PartitionSpec as P

HEAD_DIM = 64
LANDMARKS = 64
CONV_TAPS = 33
PINV_STEPS = 6
DOCS = 8
PER_DOC = LANDMARKS // DOCS
SEQ_LEN = 1024
EPSILON = 1e-05
SCALE = HEAD_DIM ** -0.5
HALF = CONV_TAPS // 2
BLOCK = 128
WINDOW = 256
F32 = jnp.float32
BF16 = jnp.bfloat16
NN = (((1,), (0,)), ((), ()))
NT = (((1,), (1,)), ((), ()))
TN = (((0,), (0,)), ((), ()))


def mm(left, right, dims=NN):
    return lax.dot_general(left, right, dims, preferred_element_type=F32)


def split(value):
    high = value.astype(BF16)
    return high, (value - high.astype(F32)).astype(BF16)


def mm3(left, right, dims=NN):
    lh, ll = left
    rh, rl = right
    return mm(lh, rh, dims) + mm(ll, rh, dims) + mm(lh, rl, dims)


def iota(shape, dim):
    return lax.broadcasted_iota(jnp.int32, shape, dim)


def head_count(width):
    return width // HEAD_DIM


def block_mask(heads):
    shape = (heads * LANDMARKS, heads * HEAD_DIM)
    return iota(shape, 0) // LANDMARKS == iota(shape, 1) // HEAD_DIM


def spread(rows, heads):
    return jnp.where(block_mask(heads), jnp.concatenate([rows] * heads, axis=0), 0.0)


def fold(full, heads):
    return jnp.concatenate(
        [full[h * 64 : (h + 1) * 64, h * 64 : (h + 1) * 64] for h in range(heads)], axis=0
    )


def stack(rows, heads):
    return jnp.concatenate([rows[:, h * 64 : (h + 1) * 64] for h in range(heads)], axis=0)


def unstack(rows, heads):
    return jnp.concatenate([rows[h * 64 : (h + 1) * 64] for h in range(heads)], axis=1)


def block_diag(rows, heads):
    return jnp.where(block_mask(heads), jnp.concatenate([rows] * heads, axis=1), 0.0)


def doc_masks(segment):
    return [jnp.broadcast_to(segment == d, (PER_DOC, segment.shape[1])) for d in range(DOCS)]


def pick(full, masks, heads):
    out = []
    for h in range(heads):
        kept = jnp.zeros(masks[0].shape, F32)
        for d in range(DOCS):
            row = h * LANDMARKS + d * PER_DOC
            kept = jnp.where(masks[d], full[row : row + PER_DOC], kept)
        out.append(kept)
    return out


def place(compact, masks, heads):
    return jnp.concatenate(
        [jnp.where(masks[d], compact[h], 0.0) for h in range(heads) for d in range(DOCS)], axis=0
    )


def per_doc(rows, masks):
    out = jnp.zeros(masks[0].shape, F32)
    for d in range(DOCS):
        out = jnp.where(masks[d], rows[d * PER_DOC : (d + 1) * PER_DOC], out)
    return out


def rows_to_lanes(full, scratch, heads):
    rows = heads * LANDMARKS
    lane_doc = (iota((rows, 128), 1) // PER_DOC) % DOCS
    row_doc = (iota((rows, 128), 0) // PER_DOC) % DOCS
    kept = jnp.where(lane_doc == row_doc, full, 0.0)
    for shift in (8, 16, 32):
        kept = kept + pltpu.roll(kept, shift, 1)
    scratch[0:rows, :] = kept
    count = heads * DOCS
    group = iota((count, 128), 1) // PER_DOC
    out = jnp.zeros((count, 128), F32)
    for i in range(PER_DOC):
        out = jnp.where(group == i, scratch[pl.ds(i, count, stride=PER_DOC), :], out)
    return jnp.concatenate([out, jnp.zeros((128 - count, 128), F32)], axis=0).T[0:64]


def lanes_to_rows(blocks, heads):
    full = jnp.concatenate([blocks, jnp.zeros((64, 128), F32)], axis=0).T
    return full[0 : heads * DOCS]


def apply_blocks(coef, operand_ref, result_ref, heads, transposed):
    count = heads * DOCS
    pieces = [operand_ref[pl.ds(j, count, stride=PER_DOC), :] for j in range(PER_DOC)]
    for i in range(PER_DOC):
        total = jnp.zeros(pieces[0].shape, F32)
        for j in range(PER_DOC):
            k = j * PER_DOC + i if transposed else i * PER_DOC + j
            total = total + coef[:, k : k + 1] * pieces[j]
        result_ref[pl.ds(i, count, stride=PER_DOC), :] = total


def bm(left, right):
    a = left.reshape(8, 8, -1)
    b = right.reshape(8, 8, -1)
    total = a[:, 0:1] * b[0:1]
    for k in range(1, 8):
        total = total + a[:, k : k + 1] * b[k : k + 1]
    return total.reshape(64, -1)


def bm_tn(left, right):
    rows = []
    for i in range(8):
        total = left[i : i + 1] * right[0:8]
        for k in range(1, 8):
            total = total + left[k * 8 + i : k * 8 + i + 1] * right[k * 8 : k * 8 + 8]
        rows.append(total)
    return jnp.concatenate(rows, axis=0)


def flip(blocks, scratch):
    scratch[0:64, :] = blocks
    return jnp.concatenate([scratch[pl.ds(i, 8, stride=8), :] for i in range(8)], axis=0)


def lane_eye():
    row = iota((64, 128), 0)
    return jnp.where(row // 8 == row % 8, 1.0, 0.0)


def column_sums(blocks):
    total = blocks[0:8]
    for i in range(1, 8):
        total = total + blocks[i * 8 : i * 8 + 8]
    return total


def row_sums(blocks):
    return jnp.concatenate(
        [jnp.sum(blocks[i * 8 : i * 8 + 8], axis=0, keepdims=True) for i in range(8)], axis=0
    )


def head_lanes(h):
    return iota((8, 128), 1) // DOCS == h


def head_most(sums, heads):
    out = jnp.ones((1, 128), F32)
    for h in range(heads):
        mask = head_lanes(h)
        most = jnp.max(jnp.max(jnp.where(mask, sums, -1e30), axis=1, keepdims=True), axis=0, keepdims=True)
        out = jnp.where(mask[0:1], most, out)
    return out


def head_total(values, heads):
    out = jnp.zeros((1, 128), F32)
    for h in range(heads):
        mask = head_lanes(h)
        total = jnp.sum(jnp.sum(jnp.where(mask, values, 0.0), axis=1, keepdims=True), axis=0, keepdims=True)
        out = jnp.where(mask[0:1], total, out)
    return out


def same_document(segment, seg_pad, start):
    rows = jnp.broadcast_to(segment[:, start : start + BLOCK], (BLOCK, BLOCK)).T
    return jnp.concatenate([rows, rows], axis=1) == seg_pad[0:1, start : start + WINDOW]


def toeplitz(taps_row):
    return pltpu.roll(jnp.broadcast_to(taps_row, (BLOCK, WINDOW)), 0, 1, stride=1, stride_axis=0)


def attend_forward_kernel(
    where_ref, tokens_ref, wq_ref, wk_ref, wv_ref, bq_ref, bv_ref, taps_ref, w_out_ref, seg_ref, mark_ref,
    keep_ref, send_ref, q_ref, k_ref, v_ref, att_ref, p1_ref, p3_ref, qm_ref, km_ref, ctx_ref, bl_ref, count_ref, mid_ref, steps_ref,
    padded, seg_pad, scratch, band,
):
    width = wq_ref.shape[0]
    heads = head_count(width)
    tokens = tokens_ref.at[0]
    rows = 256

    def project(i, carry):
        at = pl.ds(pl.multiple_of(i * rows, rows), rows)
        x = tokens[at, :]
        q_ref[at, :] = (mm(x, wq_ref[...], NT) + bq_ref[...]).astype(BF16)
        k_ref[at, :] = mm(x, wk_ref[...], NT).astype(BF16)
        value = (mm(x, wv_ref[...], NT) + bv_ref[...]).astype(BF16)
        v_ref[at, :] = value
        padded[pl.ds(pl.multiple_of(i * rows + HALF, 16), rows), :] = value
        return carry

    padded[0:HALF, :] = jnp.zeros((HALF, width), BF16)
    padded[SEQ_LEN + HALF :, :] = jnp.zeros((WINDOW - HALF, width), BF16)
    lax.fori_loop(0, SEQ_LEN // rows, project, 0)

    segment = seg_ref[0].astype(F32)
    masks = doc_masks(segment)
    one_hot = mark_ref[0] == iota((LANDMARKS, SEQ_LEN), 0)
    counts = jnp.sum(one_hot.astype(F32), axis=1, keepdims=True)
    pool = one_hot.astype(BF16)
    q_marks = mm(pool, q_ref[...]) / counts
    k_marks = mm(pool, k_ref[...]) / counts
    count_ref[...] = jnp.broadcast_to(counts, (LANDMARKS, 128))
    qm_ref[...] = q_marks
    km_ref[...] = k_marks
    k_block = split(spread(k_marks, heads))
    q_wide = spread(q_marks, heads)
    q_block = split(q_wide)

    queries = q_ref[...]
    scores = pick(mm(k_block[0], queries, NT) + mm(k_block[1], queries, NT), masks, heads)
    first = []
    for h in range(heads):
        s = scores[h] * SCALE
        e = jnp.exp(s - jnp.max(s, axis=0, keepdims=True))
        first.append(e / jnp.sum(e, axis=0, keepdims=True))
    p1_ref[...] = jnp.concatenate(first, axis=0)

    keys = k_ref[...]
    scores = pick(mm(q_block[0], keys, NT) + mm(q_block[1], keys, NT), masks, heads)
    last = []
    for h in range(heads):
        s = scores[h] * SCALE
        most = jnp.concatenate(
            [jnp.max(jnp.where(masks[d], s, -1e30), axis=1, keepdims=True) for d in range(DOCS)], axis=0
        )
        e = jnp.exp(s - per_doc(most, masks))
        total = jnp.concatenate(
            [jnp.sum(jnp.where(masks[d], e, 0.0), axis=1, keepdims=True) for d in range(DOCS)], axis=0
        )
        last.append(e / per_doc(total, masks))
    p3_ref[...] = jnp.concatenate(last, axis=0)

    weights = split(place(last, masks, heads))
    values = v_ref[...]
    context = fold(mm(weights[0], values) + mm(weights[1], values), heads)
    ctx_ref[...] = context

    twice = jnp.concatenate([k_marks, k_marks], axis=0)
    grid = lax.dot_general(q_wide, twice, NT, precision=lax.Precision.HIGHEST, preferred_element_type=F32)
    scores = (rows_to_lanes(grid, scratch, heads) * SCALE).reshape(8, 8, 128)
    e = jnp.exp(scores - jnp.max(scores, axis=1, keepdims=True))
    middle = (e / jnp.sum(e, axis=1, keepdims=True)).reshape(64, 128)
    used = iota((64, 128), 1) < heads * DOCS
    middle = jnp.where(used, middle, 0.0)
    mid_ref[...] = middle
    norm = head_most(column_sums(middle), heads) * head_most(row_sums(middle), heads)
    eye = lane_eye()

    def step(n, inverse):
        product = bm(middle, inverse)
        second = 15.0 * eye - bm(product, 7.0 * eye - product)
        third = 13.0 * eye - bm(product, second)
        steps_ref[n, 0] = inverse
        steps_ref[n, 1] = product
        steps_ref[n, 2] = second
        steps_ref[n, 3] = third
        return 0.25 * bm(inverse, third)

    inverse = lax.fori_loop(0, PINV_STEPS, step, flip(middle, scratch) / norm)
    steps_ref[PINV_STEPS, 0] = inverse
    coef = lanes_to_rows(inverse, heads)
    apply_blocks(coef, ctx_ref, bl_ref, heads, False)
    blended = split(block_diag(bl_ref[...], heads))
    weights = split(place(first, masks, heads))
    attended = mm3(weights, blended, TN)

    for h in range(heads):
        tap = split(toeplitz(taps_ref[h : h + 1, :]))
        band[h, 0] = tap[0]
        band[h, 1] = tap[1]
    seg_pad[:, 0:128] = jnp.zeros((8, 128), F32)
    seg_pad[:, 0:SEQ_LEN] = jnp.broadcast_to(pltpu.roll(segment, HALF, 1), (8, SEQ_LEN))
    seg_pad[:, SEQ_LEN:] = jnp.broadcast_to(segment[:, SEQ_LEN - 1 : SEQ_LEN], (8, WINDOW))
    att_ref[...] = attended.astype(BF16)
    lane_head = iota((BLOCK, width), 1) // HEAD_DIM
    scratch_f = attended

    for b in range(SEQ_LEN // BLOCK):
        start = b * BLOCK
        rows_at = pl.ds(start, BLOCK)
        same = same_document(segment, seg_pad, start)
        window = padded[pl.ds(start, WINDOW), :]
        total = scratch_f[start : start + BLOCK]
        for h in range(heads):
            part = mm(jnp.where(same, band[h, 0], 0), window) + mm(jnp.where(same, band[h, 1], 0), window)
            total = total + jnp.where(lane_head == h, part, 0.0)
        att_ref[rows_at, :] = total.astype(BF16)

    half = SEQ_LEN // 2
    core = where_ref[1]
    weight = w_out_ref[...]
    for i in range(half // rows):
        at = pl.ds(pl.multiple_of(core * half + i * rows, rows), rows)
        keep_ref[i * rows : (i + 1) * rows, :] = mm(att_ref[at, :], weight).astype(BF16)
        at = pl.ds(pl.multiple_of((1 - core) * half + i * rows, rows), rows)
        send_ref[i * rows : (i + 1) * rows, :] = mm(att_ref[at, :], weight).astype(BF16)


def attend_forward(where, tokens, wq, wk, wv, bq, bv, taps, w_out, segments, marks):
    dim = tokens.shape[2]
    width = wq.shape[0]
    heads = head_count(width)
    half = SEQ_LEN // 2

    def whole(*shape):
        return pl.BlockSpec(shape, lambda i, w: (0,) * len(shape))

    def one(*shape):
        return pl.BlockSpec((1,) + shape, lambda i, w: (w[0],) + (0,) * len(shape))

    outs = [
        ((half, dim), BF16), ((half, dim), BF16),
        ((SEQ_LEN, width), BF16), ((SEQ_LEN, width), BF16), ((SEQ_LEN, width), BF16), ((SEQ_LEN, width), BF16),
        ((heads * 8, SEQ_LEN), F32), ((heads * 8, SEQ_LEN), F32),
        ((LANDMARKS, width), F32), ((LANDMARKS, width), F32),
        ((heads * LANDMARKS, HEAD_DIM), F32), ((heads * LANDMARKS, HEAD_DIM), F32),
        ((LANDMARKS, 128), F32), ((64, 128), F32), ((PINV_STEPS + 1, 4, 64, 128), F32),
    ]
    return pl.pallas_call(
        attend_forward_kernel,
        out_shape=[jax.ShapeDtypeStruct(s, t) for s, t in outs],
        grid_spec=pltpu.PrefetchScalarGridSpec(
            num_scalar_prefetch=1,
            grid=(1,),
            in_specs=[
                one(SEQ_LEN, dim), whole(width, dim), whole(width, dim), whole(width, dim), whole(1, width), whole(1, width),
                whole(heads, WINDOW), whole(width, dim), one(1, SEQ_LEN), one(1, SEQ_LEN),
            ],
            out_specs=[whole(*s) for s, t in outs],
            scratch_shapes=[
                pltpu.VMEM((SEQ_LEN + WINDOW, width), BF16),
                pltpu.VMEM((8, SEQ_LEN + WINDOW), F32),
                pltpu.VMEM((heads * LANDMARKS, 128), F32),
                pltpu.VMEM((heads, 2, BLOCK, WINDOW), BF16),
            ],
        ),
        compiler_params=pltpu.CompilerParams(vmem_limit_bytes=56 << 20),
        cost_estimate=pl.CostEstimate(flops=6_000_000_000, bytes_accessed=8_000_000, transcendentals=100_000),
    )(where, tokens, wq, wk, wv, bq, bv, taps, w_out, segments, marks)


def diagonal_sums(band):
    row = iota(band.shape, 0)
    for bit in range(7):
        shift = 1 << bit
        moved = pltpu.roll(band, WINDOW - shift, 1)
        band = jnp.where((row // shift) % 2 == 1, moved, band)
    return jnp.sum(band, axis=0, keepdims=True)


def attend_backward_kernel(
    where_ref, mine_ref, theirs_ref, tokens_ref, wq_ref, wk_ref, wv_ref, taps_ref, w_out_ref, seg_ref, mark_ref,
    q_ref, k_ref, v_ref, att_ref, p1_ref, p3_ref, qm_ref, km_ref, ctx_ref, bl_ref, count_ref, mid_ref, steps_ref, prev_ref, prev_small_ref,
    keep_ref, send_ref, weights_ref, small_ref,
    grad_ref, up_ref, value_ref, seg_pad, scratch, scratch_b, band, corr, dbl_ref, dctx_ref, dqm_ref, dkm_ref, stack_ref, dq_ref, dk_ref, dv_ref,
):
    width = wq_ref.shape[0]
    heads = head_count(width)
    half = SEQ_LEN // 2
    core = where_ref[1]
    other = 1 - core
    rows = 256

    grad_ref[0:HALF, :] = jnp.zeros((HALF, width), F32)
    grad_ref[SEQ_LEN + HALF :, :] = jnp.zeros((WINDOW - HALF, width), F32)
    value_ref[0:HALF, :] = jnp.zeros((HALF, width), BF16)
    value_ref[SEQ_LEN + HALF :, :] = jnp.zeros((WINDOW - HALF, width), BF16)
    value_ref[HALF : SEQ_LEN + HALF, :] = v_ref[...]
    for i in range(half // rows):
        at = pl.ds(i * rows, rows)
        to = pl.multiple_of(core * half + i * rows, rows)
        up_ref[pl.ds(to, rows), :] = mine_ref[at, :]
        grad_ref[pl.ds(to + HALF, rows), :] = mm(mine_ref[at, :], w_out_ref[...], NT)
        to = pl.multiple_of(other * half + i * rows, rows)
        up_ref[pl.ds(to, rows), :] = theirs_ref[at, :]
        grad_ref[pl.ds(to + HALF, rows), :] = mm(theirs_ref[at, :], w_out_ref[...], NT)
    attended_grad = mm(att_ref[...], up_ref[...], TN)
    weights_ref[3 * width : 4 * width, :] = prev_ref[3 * width : 4 * width, :] + attended_grad

    segment = seg_ref[0].astype(F32)
    masks = doc_masks(segment)
    pool = (mark_ref[0] == iota((LANDMARKS, SEQ_LEN), 0)).astype(BF16)
    first = [p1_ref[h * 8 : h * 8 + 8, :] for h in range(heads)]
    last = [p3_ref[h * 8 : h * 8 + 8, :] for h in range(heads)]
    gradient = split(grad_ref[HALF : SEQ_LEN + HALF, :])
    values = v_ref[...]
    queries = q_ref[...]
    keys = k_ref[...]

    first_wide = split(place(first, masks, heads))
    dbl = fold(mm3(first_wide, gradient), heads)
    dbl_ref[...] = dbl
    blended = split(block_diag(bl_ref[...], heads))
    dfirst = pick(mm3(blended, gradient, NT), masks, heads)
    dscore = [
        SCALE * first[h] * (dfirst[h] - jnp.sum(first[h] * dfirst[h], axis=0, keepdims=True)) for h in range(heads)
    ]
    dscore_one = split(place(dscore, masks, heads))
    dkm = fold(mm(dscore_one[0], queries) + mm(dscore_one[1], queries), heads)

    inverse = steps_ref[PINV_STEPS, 0]
    apply_blocks(lanes_to_rows(inverse, heads), dbl_ref, dctx_ref, heads, True)
    dctx = dctx_ref[...]
    context = unstack(ctx_ref[...], heads)
    grid = lax.dot_general(
        block_diag(dbl, heads), jnp.concatenate([context, context], axis=0), NT,
        precision=lax.Precision.HIGHEST, preferred_element_type=F32,
    )
    dinverse = rows_to_lanes(grid, scratch, heads)
    middle = mid_ref[...]
    eye = lane_eye()

    def step(n, carry):
        dz, dmid = carry
        n = PINV_STEPS - 1 - n
        z = steps_ref[n, 0]
        product = steps_ref[n, 1]
        second = steps_ref[n, 2]
        third = steps_ref[n, 3]
        dthird = 0.25 * bm_tn(z, dz)
        dz_next = 0.25 * bm(dz, flip(third, scratch_b.at[0]))
        dsecond = -bm_tn(product, dthird)
        dprod = -bm(dthird, flip(second, scratch_b.at[1])) - bm(dsecond, flip(7.0 * eye - product, scratch_b.at[2]))
        dprod = dprod + bm_tn(product, dsecond)
        dmid = dmid + bm(dprod, flip(z, scratch_b.at[3]))
        dz_next = dz_next + bm_tn(middle, dprod)
        return dz_next, dmid

    dz, dmid = lax.fori_loop(0, PINV_STEPS, step, (dinverse, jnp.zeros((64, 128), F32)))
    columns = column_sums(middle)
    across = row_sums(middle)
    column_most = head_most(columns, heads)
    row_most = head_most(across, heads)
    start = flip(middle, scratch) / (column_most * row_most)
    dmid = dmid + flip(dz, scratch) / (column_most * row_most)
    total = jnp.sum(dz * start, axis=0, keepdims=True)
    total = head_total(jnp.where(iota((8, 128), 0) == 0, jnp.broadcast_to(total, (8, 128)), 0.0), heads)
    hit = jnp.where(columns == column_most, 1.0, 0.0)
    dcolumns = -total / column_most * hit / jnp.maximum(head_total(hit, heads), 1.0)
    hit = jnp.where(across == row_most, 1.0, 0.0)
    drows = -total / row_most * hit / jnp.maximum(head_total(hit, heads), 1.0)
    dmid = dmid + jnp.concatenate([dcolumns + drows[i : i + 1] for i in range(8)], axis=0)
    dgrid = jnp.concatenate(
        [
            SCALE * middle[i * 8 : i * 8 + 8]
            * (dmid[i * 8 : i * 8 + 8] - jnp.sum(middle[i * 8 : i * 8 + 8] * dmid[i * 8 : i * 8 + 8], axis=0, keepdims=True))
            for i in range(8)
        ],
        axis=0,
    )
    coef = lanes_to_rows(dgrid, heads)
    q_stack = stack(qm_ref[...], heads)
    k_stack = stack(km_ref[...], heads)
    stack_ref[...] = k_stack
    apply_blocks(coef, stack_ref, dqm_ref, heads, False)
    stack_ref[...] = q_stack
    apply_blocks(coef, stack_ref, dkm_ref, heads, True)

    dctx_wide = split(block_diag(dctx, heads))
    dlast = pick(mm(dctx_wide[0], values, NT) + mm(dctx_wide[1], values, NT), masks, heads)
    inner = jnp.sum(dctx * ctx_ref[...], axis=1, keepdims=True)
    dscore = [
        SCALE * last[h] * (dlast[h] - per_doc(inner[h * 64 : (h + 1) * 64], masks)) for h in range(heads)
    ]
    dscore_last = split(place(dscore, masks, heads))
    dqm = fold(mm(dscore_last[0], keys) + mm(dscore_last[1], keys), heads) + dqm_ref[...]
    dkm = dkm + dkm_ref[...]
    counts = count_ref[:, 0:1]
    dqm = split(unstack(dqm, heads) / counts)
    dkm = split(unstack(dkm, heads) / counts)
    k_wide = split(spread(km_ref[...], heads))
    q_wide = split(spread(qm_ref[...], heads))

    def pulled(scores, wide, marks):
        left = jnp.concatenate([scores[0], pool], axis=0)
        return (
            mm(left, jnp.concatenate([wide[0], marks[0]], axis=0), TN)
            + mm(left, jnp.concatenate([wide[1], marks[1]], axis=0), TN)
            + mm(scores[1], wide[0], TN)
        )

    dq_ref[...] = pulled(dscore_one, k_wide, dqm).astype(BF16)
    dk_ref[...] = pulled(dscore_last, q_wide, dkm).astype(BF16)
    last_wide = split(place(last, masks, heads))
    dvalue = mm3(last_wide, dctx_wide, TN)

    for h in range(heads):
        tap = split(toeplitz(taps_ref[h : h + 1, :]))
        band[h, 0] = tap[0]
        band[h, 1] = tap[1]
        corr[h] = jnp.zeros((BLOCK, WINDOW), F32)
    seg_pad[:, 0:128] = jnp.zeros((8, 128), F32)
    seg_pad[:, 0:SEQ_LEN] = jnp.broadcast_to(pltpu.roll(segment, HALF, 1), (8, SEQ_LEN))
    seg_pad[:, SEQ_LEN:] = jnp.broadcast_to(segment[:, SEQ_LEN - 1 : SEQ_LEN], (8, WINDOW))
    lane_head = iota((BLOCK, width), 1) // HEAD_DIM
    for b in range(SEQ_LEN // BLOCK):
        begin = b * BLOCK
        same = same_document(segment, seg_pad, begin)
        window = split(grad_ref[begin : begin + WINDOW, :])
        near = value_ref[begin : begin + WINDOW, :]
        block = split(grad_ref[begin + HALF : begin + HALF + BLOCK, :])
        total = dvalue[begin : begin + BLOCK]
        for h in range(heads):
            taps = jnp.where(same, band[h, 0], 0)
            part = mm(taps, window[0]) + mm(taps, window[1]) + mm(jnp.where(same, band[h, 1], 0), window[0])
            total = total + jnp.where(lane_head == h, part, 0.0)
            mine = lane_head == h
            part = mm(jnp.where(mine, block[0], 0), near, NT) + mm(jnp.where(mine, block[1], 0), near, NT)
            corr[h] = corr[h] + jnp.where(same, part, 0.0)
        dv_ref[begin : begin + BLOCK, :] = total.astype(BF16)

    small_ref[...] = prev_small_ref[...]
    for h in range(heads):
        small_ref[h : h + 1, :] = prev_small_ref[h : h + 1, :] + diagonal_sums(corr[h])
    small_ref[heads : heads + 1, 0:width] = prev_small_ref[heads : heads + 1, 0:width] + jnp.sum(
        dq_ref[...].astype(F32), axis=0, keepdims=True
    )
    small_ref[heads + 1 : heads + 2, 0:width] = prev_small_ref[heads + 1 : heads + 2, 0:width] + jnp.sum(
        dv_ref[...].astype(F32), axis=0, keepdims=True
    )
    tokens = tokens_ref[0]
    for n, ref in enumerate((dq_ref, dk_ref, dv_ref)):
        at = pl.ds(n * width, width)
        weights_ref[at, :] = prev_ref[at, :] + mm(ref[...], tokens, TN)

    for i in range(half // rows):
        for base, out_ref in ((core, keep_ref), (other, send_ref)):
            at = pl.ds(pl.multiple_of(base * half + i * rows, rows), rows)
            out_ref[i * rows : (i + 1) * rows, :] = (
                mm(dq_ref[at, :], wq_ref[...]) + mm(dk_ref[at, :], wk_ref[...]) + mm(dv_ref[at, :], wv_ref[...])
            ).astype(BF16)


def attend_backward(where, mine, theirs, tokens, wq, wk, wv, taps, w_out, segments, marks, saved, prev, prev_small):
    dim = tokens.shape[2]
    width = wq.shape[0]
    heads = head_count(width)
    half = SEQ_LEN // 2

    def whole(*shape):
        return pl.BlockSpec(shape, lambda i, w: (0,) * len(shape))

    def one(*shape):
        return pl.BlockSpec((1,) + shape, lambda i, w: (w[0],) + (0,) * len(shape))

    outs = [((half, dim), BF16), ((half, dim), BF16), ((4 * width, dim), F32), ((8, WINDOW), F32)]
    return pl.pallas_call(
        attend_backward_kernel,
        out_shape=[jax.ShapeDtypeStruct(s, t) for s, t in outs],
        grid_spec=pltpu.PrefetchScalarGridSpec(
            num_scalar_prefetch=1,
            grid=(1,),
            in_specs=[
                whole(half, dim), whole(half, dim), one(SEQ_LEN, dim),
                whole(width, dim), whole(width, dim), whole(width, dim),
                whole(heads, WINDOW), whole(width, dim), one(1, SEQ_LEN), one(1, SEQ_LEN),
                *[whole(*s.shape) for s in saved], whole(4 * width, dim), whole(8, WINDOW),
            ],
            out_specs=[whole(*s) for s, t in outs],
            scratch_shapes=[
                pltpu.VMEM((SEQ_LEN + WINDOW, width), F32),
                pltpu.VMEM((SEQ_LEN, dim), BF16),
                pltpu.VMEM((SEQ_LEN + WINDOW, width), BF16),
                pltpu.VMEM((8, SEQ_LEN + WINDOW), F32),
                pltpu.VMEM((heads * LANDMARKS, 128), F32),
                pltpu.VMEM((4, 64, 128), F32),
                pltpu.VMEM((heads, 2, BLOCK, WINDOW), BF16),
                pltpu.VMEM((heads, BLOCK, WINDOW), F32),
                *[pltpu.VMEM((heads * LANDMARKS, HEAD_DIM), F32)] * 5,
                *[pltpu.VMEM((SEQ_LEN, width), BF16)] * 3,
            ],
        ),
        compiler_params=pltpu.CompilerParams(vmem_limit_bytes=60 << 20),
        cost_estimate=pl.CostEstimate(flops=12_000_000_000, bytes_accessed=14_000_000, transcendentals=100_000),
    )(where, mine, theirs, tokens, wq, wk, wv, taps, w_out, segments, marks, *saved, prev, prev_small)


ERFC = (
    0.12694266047513267, 0.12694157407364748, 0.11413597639508828, 0.08762459251766126, 0.05998263605520133,
    -0.01120062503236582, 0.07123816174906503, -0.1503297151041413, 0.09536518640917925, -0.020700440227622966,
)


def normal_cdf(value):
    size = jnp.abs(value)
    t = 1.0 / (1.0 + 0.31819805153394637 * size)
    poly = ERFC[-1]
    for coef in ERFC[-2::-1]:
        poly = poly * t + coef
    bell = jnp.exp(-0.5 * size * size)
    tail = bell * (t * poly)
    return jnp.where(value > 0.0, 1.0 - tail, tail), bell


def up_down_kernel(one_ref, two_ref, w_up_ref, b_up_ref, w_down_ref, *outs):
    for n, ref in enumerate((one_ref, two_ref)):
        act_ref, slope_ref, part_ref = outs[3 * n : 3 * n + 3]
        hidden = mm(ref[...], w_up_ref[...]) + b_up_ref[...]
        below, bell = normal_cdf(hidden)
        act = (hidden * below).astype(BF16)
        act_ref[...] = act
        slope_ref[...] = (below + hidden * (bell * 0.3989422804014327)).astype(BF16)
        part_ref[...] = mm(act, w_down_ref[...]).astype(BF16)


def up_down(one, two, w_up, b_up, w_down):
    rows, dim = one.shape
    units = w_up.shape[1]
    step = 128
    block = pl.BlockSpec((step, dim), lambda i: (i, 0))
    wide = pl.BlockSpec((step, units), lambda i: (i, 0))

    def fixed(*shape):
        return pl.BlockSpec(shape, lambda i: (0, 0), pipeline_mode=pl.Buffered(1))

    shapes = [(rows, units), (rows, units), (rows, dim)] * 2
    return pl.pallas_call(
        up_down_kernel,
        out_shape=[jax.ShapeDtypeStruct(s, BF16) for s in shapes],
        grid=(rows // step,),
        in_specs=[block, block, fixed(dim, units), fixed(1, units), fixed(units, dim)],
        out_specs=[wide, wide, block] * 2,
        compiler_params=pltpu.CompilerParams(vmem_limit_bytes=40 << 20),
        cost_estimate=pl.CostEstimate(flops=8 * rows * dim * units, bytes_accessed=8_000_000, transcendentals=2 * rows * units),
    )(one, two, w_up, b_up, w_down)


def up_down_back_kernel(*refs):
    ins, rest = refs[:8], refs[8:]
    w_up_ref, w_down_ref, prev_down_ref, prev_up_ref, prev_bias_ref = rest[:5]
    part_refs, down_ref, up_ref, bias_ref = rest[5:7], rest[7], rest[8], rest[9]

    @pl.when(pl.program_id(0) == 0)
    def _():
        down_ref[...] = prev_down_ref[...]
        up_ref[...] = prev_up_ref[...]
        bias_ref[...] = prev_bias_ref[...]

    for n in range(2):
        grad_ref, act_ref, slope_ref, low_ref = ins[4 * n : 4 * n + 4]
        grad = grad_ref[...]
        hidden = (mm(grad, w_down_ref[...], NT) * slope_ref[...].astype(F32)).astype(BF16)
        part_refs[n][...] = mm(hidden, w_up_ref[...], NT).astype(BF16)
        down_ref[...] += mm(act_ref[...], grad, TN)
        up_ref[...] += mm(low_ref[...], hidden, TN)
        bias_ref[0:1, :] += jnp.sum(hidden.astype(F32), axis=0, keepdims=True)


def up_down_back(one, two, w_up, w_down, prev):
    rows, dim = one[0].shape
    units = w_up.shape[1]
    step = 256
    block = pl.BlockSpec((step, dim), lambda i: (i, 0))
    wide = pl.BlockSpec((step, units), lambda i: (i, 0))

    def fixed(*shape):
        return pl.BlockSpec(shape, lambda i: (0, 0), pipeline_mode=pl.Buffered(1))

    return pl.pallas_call(
        up_down_back_kernel,
        out_shape=[
            jax.ShapeDtypeStruct((rows, dim), BF16), jax.ShapeDtypeStruct((rows, dim), BF16),
            jax.ShapeDtypeStruct((units, dim), F32), jax.ShapeDtypeStruct((dim, units), F32), jax.ShapeDtypeStruct((8, units), F32),
        ],
        grid=(rows // step,),
        in_specs=[block, wide, wide, block] * 2
        + [fixed(dim, units), fixed(units, dim), fixed(units, dim), fixed(dim, units), fixed(8, units)],
        out_specs=[block, block, fixed(units, dim), fixed(dim, units), fixed(8, units)],
        compiler_params=pltpu.CompilerParams(vmem_limit_bytes=56 << 20),
        cost_estimate=pl.CostEstimate(flops=16 * rows * dim * units, bytes_accessed=16_000_000, transcendentals=0),
    )(*one, *two, w_up, w_down, *prev)


def swap(value, mask, axis="tensor"):
    count = lax.axis_size(axis)
    return lax.ppermute(value, axis, [(i, i ^ mask) for i in range(count)])


def gather_blocks(mine):
    near = swap(mine, 1)
    far = swap(mine, 2)
    return mine, near, far, swap(far, 1)


def reduce_blocks(mine, near, far, cross):
    through = swap(far + swap(cross, 1), 2)
    return mine.astype(F32) + swap(near, 1).astype(F32) + through.astype(F32)


def normalize(value):
    centered = value - jnp.mean(value, axis=-1, keepdims=True)
    inv = lax.rsqrt(jnp.mean(centered * centered, axis=-1, keepdims=True) + EPSILON)
    return centered * inv, inv


def norm_back(grad, gain, unit, inv):
    r = grad * gain
    back = (r - jnp.mean(r, axis=-1, keepdims=True) - unit * jnp.mean(r * unit, axis=-1, keepdims=True)) * inv
    return back, jnp.sum(grad * unit, axis=0), jnp.sum(grad, axis=0)


def per_device(
    tokens, w_query, w_key, w_value, b_query, b_value, conv_taps, w_out, b_out, gain_one, shift_one, w_up, b_up, w_down,
    b_down, gain_two, shift_two, cotangent, segment_ids, landmark_ids,
):
    dim = tokens.shape[1]
    width = w_query.shape[1]
    heads = head_count(width)
    seqs = tokens.shape[0] // SEQ_LEN
    me = lax.axis_index("tensor")
    core, chip = me % 2, me // 2
    own_rows = cotangent.shape[0]
    sequences = tokens.reshape(seqs, SEQ_LEN, dim)
    segments = segment_ids.reshape(seqs, 1, SEQ_LEN)
    marks = landmark_ids.reshape(seqs, 1, SEQ_LEN)
    at_own = jnp.stack([chip, core]).astype(jnp.int32)
    at_far = jnp.stack([1 - chip, core]).astype(jnp.int32)
    taps = jnp.pad(conv_taps, ((0, 0), (0, WINDOW - CONV_TAPS)))
    taps_back = jnp.pad(conv_taps[:, ::-1], ((0, 0), (0, WINDOW - CONV_TAPS)))
    wq, wk, wv = w_query.T, w_key.T, w_value.T

    def forward(at):
        return attend_forward(
            at, sequences, wq, wk, wv, b_query[None], b_value[None], taps, w_out, segments, marks
        )

    far = forward(at_far)
    own = forward(at_own)
    summed = reduce_blocks(own[0], own[1], far[0], far[1])
    own_tokens = lax.dynamic_slice_in_dim(tokens, me * own_rows, own_rows, 0).astype(F32)
    unit_one, inv_one = normalize(own_tokens + summed + b_out)
    normed = unit_one * gain_one + shift_one
    low = gather_blocks(normed.astype(BF16))
    bias = b_up[None]
    fwd_own = up_down(low[0], low[1], w_up, bias, w_down)
    fwd_far = up_down(low[2], low[3], w_up, bias, w_down)
    branch = reduce_blocks(fwd_own[2], fwd_own[5], fwd_far[2], fwd_far[5])
    unit_two, inv_two = normalize(normed + branch + b_down)
    output = (unit_two * gain_two + shift_two).astype(BF16)
    grad_pre_out, grad_gain_two, grad_shift_two = norm_back(cotangent.astype(F32), gain_two, unit_two, inv_two)
    grad_b_down = jnp.sum(grad_pre_out, axis=0)
    grad = gather_blocks(grad_pre_out.astype(BF16))
    units = w_up.shape[1]
    zero = (jnp.zeros((units, dim), F32), jnp.zeros((dim, units), F32), jnp.zeros((8, units), F32))
    back_own = up_down_back(
        (grad[0], fwd_own[0], fwd_own[1], low[0]), (grad[1], fwd_own[3], fwd_own[4], low[1]), w_up, w_down, zero
    )
    back_far = up_down_back(
        (grad[2], fwd_far[0], fwd_far[1], low[2]), (grad[3], fwd_far[3], fwd_far[4], low[3]), w_up, w_down, back_own[2:]
    )
    back_normed = reduce_blocks(back_own[0], back_own[1], back_far[0], back_far[1])
    grad_pre_norm, grad_gain_one, grad_shift_one = norm_back(grad_pre_out + back_normed, gain_one, unit_one, inv_one)
    grad_b_out = jnp.sum(grad_pre_norm, axis=0)
    up = gather_blocks(grad_pre_norm.astype(BF16))
    ffn_sum = lax.psum(jnp.concatenate([back_far[2], back_far[3]], axis=0).astype(BF16), "dp")

    def backward(at, mine, theirs, saved, prev, prev_small):
        return attend_backward(
            at, mine, theirs, sequences, wq, wk, wv, taps_back, w_out, segments, marks, saved, prev, prev_small
        )

    none = (jnp.zeros((4 * width, dim), F32), jnp.zeros((8, WINDOW), F32))
    first = backward(at_own, up[0], up[1], own[2:], *none)
    second = backward(at_far, up[2], up[3], far[2:], first[2], first[3])
    input_grad = grad_pre_norm + reduce_blocks(first[0], first[1], second[0], second[1])
    attend_sum, ffn_sum = lax.optimization_barrier((second[2].astype(BF16), ffn_sum))
    attend_sum = lax.psum(attend_sum, "dp").astype(F32)
    ffn_sum = ffn_sum.astype(F32)

    norms = jnp.stack([grad_gain_one, grad_shift_one, grad_b_out, grad_gain_two, grad_shift_two, grad_b_down])
    for mask in (1, 2):
        norms = norms + swap(norms, mask)
    small = jnp.concatenate(
        [norms, back_far[4][0:1], jnp.pad(second[3][0 : heads + 2], ((0, 0), (0, dim - WINDOW)))], axis=0
    )
    mask = 1
    while mask < lax.axis_size("dp"):
        small = small + swap(small, mask, "dp")
        mask *= 2
    return (
        output,
        input_grad,
        attend_sum[0:width].T,
        attend_sum[width : 2 * width].T,
        attend_sum[2 * width : 3 * width].T,
        small[7 + heads, 0:width],
        small[8 + heads, 0:width],
        small[7 : 7 + heads, 0:CONV_TAPS],
        attend_sum[3 * width :],
        small[2],
        small[0],
        small[1],
        ffn_sum[units:],
        small[6, 0:units],
        ffn_sum[0:units],
        small[5],
        small[3],
        small[4],
    )


def solution(mesh):
    rows = P(("dp", "tensor"), None)
    columns = P(None, "tensor")
    split_rows = P("tensor", None)
    vector = P("tensor")
    return jax.shard_map(
        per_device,
        mesh=mesh,
        in_specs=(
            P("dp", None), columns, columns, columns, vector, vector, split_rows, split_rows, P(), P(), P(),
            columns, vector, split_rows, P(), P(), P(), rows, P("dp"), P("dp"),
        ),
        out_specs=(
            rows, rows, columns, columns, columns, vector, vector, split_rows, split_rows, P(), P(), P(),
            columns, vector, split_rows, P(), P(), P(),
        ),
        check_vma=False,
    )
```

time: 822 us -> 419 us (0.51)
  waiting for transfers between devices: 407 us -> 232 us
  matrix products: 169 us -> 0 us
  Pallas kernels: 0 us -> 101 us
  blocking collectives: 80.5 us -> 0 us
  other arithmetic: 92.7 us -> 21.2 us
  local copies, waits for them, and re-layouts: 45.9 us -> 22.5 us
  starting transfers between devices: 0.5 us -> 19.1 us
    dot_general x110 -> x0, matrix products: 165 us -> none  [the longest x6 29 us: contract_cols(): lax.dot_general(left, right, (((1,), (1,)), ((), ())), preferred_element_...]
    reduce_scatter x4 -> x0, waiting for transfers between devices: 158 us -> none  [the longest x1 61.1 us: per_device(): lax.psum_scatter(jnp.dot(attended, w_out, preferred_element_type=jnp.floa...]
    ppermute x0 -> x26, waiting for transfers between devices: none -> 120 us  [swap(): return lax.ppermute(value, axis, [(i, i ^ mask) for i in range(count)])]
    pallas_call x0 -> x8, Pallas kernels: none -> 101 us  [the longest x2 37.5 us: attend_backward(): pl.pallas_call(attend_backward_kernel, out_shape=[jax.ShapeDtypeStruct(s,...]
    all_gather x3 -> x0, waiting for transfers between devices: 82.7 us -> none  [the longest x1 28.7 us: per_device(): lax.all_gather(grad_pre_out.astype(jnp.bfloat16), 'tensor', axis=0, tiled...]
    psum x2 -> x0, blocking collectives: 80.5 us -> none  [the longest x1 40.6 us: per_device(): lax.psum((grad_gain_one, grad_shift_one, grad_b_out, grad_gain_two, grad_...]
    psum x1 -> x2, waiting for transfers between devices: 167 us -> 112 us  [the longest x1 58.7 us: per_device(): attend_sum = lax.psum(attend_sum, 'dp').astype(F32)]
    reduce_sum x22 -> x7, other arithmetic: 37.7 us -> 6.69 us  [the longest x2 2.53 us: normalize(): centered = value - jnp.mean(value, axis=-1, keepdims=True)]
  transfers between devices with their start and end apart: 8 -> 28, of which waited for: 7 -> 16; matrix products, arithmetic and copies ran while one was open for 5% -> 5% of each run, Pallas kernels for 0% -> 19%
where the time goes in v1:
time: 419 us; the launch traced here: 411 us
  waiting for transfers between devices  232 us (55%)
  Pallas kernels  101 us (24%)
  local copies, waits for them, and re-layouts  22.5 us (5%)
  other arithmetic  21.2 us (5%)
  starting transfers between devices  19.1 us (5%)
  between operations  15.1 us (4%)
    ppermute x26, waiting for transfers between devices, swap(): return lax.ppermute(value, axis, [(i, i ^ mask) for i in range(count)])  120 us
    psum x1, waiting for transfers between devices, per_device(): attend_sum = lax.psum(attend_sum, 'dp').astype(F32)  58.7 us
    psum x1, waiting for transfers between devices, per_device(): lax.psum(jnp.concatenate([back_far[2], back_far[3]], axis=0).astype(BF16)...  53.3 us
    pallas_call x2, Pallas kernels, attend_backward(): pl.pallas_call(attend_backward_kernel, out_shape=[jax.ShapeDtypeStruct(s,...  37.5 us
    pallas_call x2, Pallas kernels, up_down_back(): pl.pallas_call(up_down_back_kernel, out_shape=[jax.ShapeDtypeStruct((rows...  25 us
    pallas_call x2, Pallas kernels, attend_forward(): pl.pallas_call(attend_forward_kernel, out_shape=[jax.ShapeDtypeStruct(s,...  23.6 us
    ppermute x26, starting transfers between devices, swap(): return lax.ppermute(value, axis, [(i, i ^ mask) for i in range(count)])  19.1 us
    pallas_call x2, Pallas kernels, up_down(): pl.pallas_call(up_down_kernel, out_shape=[jax.ShapeDtypeStruct(s, BF16) f...  15.4 us
  transfers between devices with their start and end apart: 28, of which 16 were waited for; matrix products, arithmetic and copies ran while one was open for 5% of the time, Pallas kernels for 19%

profile of v1, /device:TPU:0, one launch (start us, length us, event | category | flops | bytes accessed | tf_op | source)
XLA Modules:
  0.0 411.2 jit_solution(6008691761084518414)
XLA Ops:
  7.3 1.3 pad.11.taps_ref
  9.1 11.7 %shard_map.332 = (bf16[512,768]{1,0:T(8,128)(2,1)}, bf16[512,768]{1,0:T(8,128)(2,1)}, bf16[1024,192]{1,0:T(8,128)(2,1)}, bf16[1024,192]{1,0:T(8,128)(2,1)}, bf16...) custom-call(s32[2]{0:T(128)} %get-tuple-element.175.where_ref, ...), custom_call_target="tpu_custom_call" | custom-call | flops 6000000000 | bytes 8000000 | tf_op jit(solution)/shard_map/pallas_call | solution.py:358
  21.4 11.9 %shard_map.331 = (bf16[512,768]{1,0:T(8,128)(2,1)}, bf16[512,768]{1,0:T(8,128)(2,1)}, bf16[1024,192]{1,0:T(8,128)(2,1)}, bf16[1024,192]{1,0:T(8,128)(2,1)}, bf16...) custom-call(s32[2]{0:T(128)} %get-tuple-element.174.where_ref, ...), custom_call_target="tpu_custom_call" | custom-call | flops 6000000000 | bytes 8000000 | tf_op jit(solution)/shard_map/pallas_call | solution.py:358
  33.6 3.0 collective-permute-start.2
  36.6 17.8 %collective-permute-done.2 = bf16[512,768]{1,0:T(8,128)(2,1)S(1)} collective-permute-done((bf16[512,768]{1,0:T(8,128)(2,1)S(1)}, bf16[512,768]{1,0:T(8,128)(2,1)S(1)}, u32[]{:S(2)}, u32[]{:S(2)}) %collective-permute-start.2) | collective-permute-done | bytes 786464 | tf_op jit(solution)/shard_map/ppermute | solution.py:715
  54.4 1.7 fusion.13
  57.1 1.8 collective-permute-start.5
  58.9 17.3 %collective-permute-done.5.one_ref.refs_3_ = bf16[512,768]{1,0:T(8,128)(2,1)S(1)} collective-permute-done((bf16[512,768]{1,0:T(8,128)(2,1)S(1)}, bf16[512,768]{1,0:T(8,128)(2,1)S(1)}, u32[]{:S(2)}, u32[]{:S(2)}) %collective-permute-start.5) | collective-permute-done | bytes 786464 | tf_op jit(solution)/shard_map/ppermute | solution.py:715
  76.7 1.8 collective-permute-done.6.two_ref.refs_7_
  78.5 7.9 %shard_map.334 = (bf16[512,768]{1,0:T(8,128)(2,1)S(1)}, bf16[512,768]{1,0:T(8,128)(2,1)S(1)}, bf16[512,768]{1,0:T(8,128)(2,1)S(1)}, bf16[512,768]{1,0:T(8,128)(2...) custom-call(bf16[512,768]{1,0:T(8,128)(2,1)S(1)} %collective-permute-done.5.one_ref.refs_3_, ...), custom_call_target="tpu_custom_call" | custom-call | flops 2415919104 | bytes 8000000 | tf_op jit(solution)/shard_map/pallas_call | solution.py:656
  89.1 0.9 copy-done.9
  90.1 7.5 %shard_map.333 = (bf16[512,768]{1,0:T(8,128)(2,1)S(1)}, bf16[512,768]{1,0:T(8,128)(2,1)S(1)}, bf16[512,768]{1,0:T(8,128)(2,1)S(1)}, bf16[512,768]{1,0:T(8,128)(2...) custom-call(bf16[512,768]{1,0:T(8,128)(2,1)S(1)} %fusion.7.one_ref.refs_3_, ...), custom_call_target="tpu_custom_call" | custom-call | flops 2415919104 | bytes 8000000 | tf_op jit(solution)/shard_map/pallas_call | solution.py:656
  98.4 1.5 collective-permute-start.8
  100.1 17.9 %collective-permute-done.8 = bf16[512,768]{1,0:T(8,128)(2,1)S(1)} collective-permute-done((bf16[512,768]{1,0:T(8,128)(2,1)S(1)}, bf16[512,768]{1,0:T(8,128)(2,1)S(1)}, u32[]{:S(2)}, u32[]{:S(2)}) %collective-permute-start.8) | collective-permute-done | bytes 786464 | tf_op jit(solution)/shard_map/ppermute | solution.py:715
  120.8 1.7 fusion.9
  122.6 1.5 collective-permute-start.11
  124.1 17.3 %collective-permute-done.11.refs_0_ = bf16[512,768]{1,0:T(8,128)(2,1)S(1)} collective-permute-done((bf16[512,768]{1,0:T(8,128)(2,1)S(1)}, bf16[512,768]{1,0:T(8,128)(2,1)S(1)}, u32[]{:S(2)}, u32[]{:S(2)}) %collective-permute-start.11) | collective-permute-done | bytes 786464 | tf_op jit(solution)/shard_map/ppermute | solution.py:715
  141.4 1.7 broadcast_3_refs_10__refs_11__prev_ref.2.refs_10_.refs_11_.prev_ref
  143.7 12.6 %shard_map.335 = (bf16[512,768]{1,0:T(8,128)(2,1)}, bf16[512,768]{1,0:T(8,128)(2,1)}, f32[768,768]{1,0:T(8,128)}, f32[768,768]{1,0:T(8,128)}, f32[8,768]{1,0:T(8,128)}) custom-call(bf16[512,768]{1,0:T(8,128)(2,1)} %copy-done.25, bf16[512,768]{1,0:T(8,128)(2,1)} %copy-done.10, bf16[512,768]{1,0:T(8,128)(2,1)} %copy-done.11, bf16[512,768]{1,0:T(8,128)(2,1)} %copy-done, ...), custom_call_target="tpu_custom_call" | custom-call | flops 4831838208 | bytes 16000000 | tf_op jit(solution)/shard_map/pallas_call | solution.py:698
  157.1 12.4 %shard_map.336 = (bf16[512,768]{1,0:T(8,128)(2,1)}, bf16[512,768]{1,0:T(8,128)(2,1)}, f32[768,768]{1,0:T(8,128)}, f32[768,768]{1,0:T(8,128)}, f32[8,768]{1,0:T(8,128)}) custom-call(bf16[512,768]{1,0:T(8,128)(2,1)} %copy-done.39, bf16[512,768]{1,0:T(8,128)(2,1)} %copy-done.6, bf16[512,768]{1,0:T(8,128)(2,1)} %copy-done.7, bf16[512,768]{1,0:T(8,128)(2,1)} %copy-done.3, ...), custom_call_target="tpu_custom_call" | custom-call | flops 4831838208 | bytes 16000000 | tf_op jit(solution)/shard_map/pallas_call | solution.py:698
  170.2 2.3 collective-permute-done.13
  172.5 1.3 add.150
  173.8 1.5 collective-permute-start.14
  175.3 18.4 %collective-permute-done.14 = bf16[512,768]{1,0:T(8,128)(2,1)S(1)} collective-permute-done((bf16[512,768]{1,0:T(8,128)(2,1)S(1)}, bf16[512,768]{1,0:T(8,128)(2,1)S(1)}, u32[]{:S(2)}, u32[]{:S(2)}) %collective-permute-start.14) | collective-permute-done | bytes 786464 | tf_op jit(solution)/shard_map/ppermute | solution.py:715
  193.7 1.1 multiply_reduce_fusion
  195.3 1.1 copy-done.14
  196.5 1.5 collective-permute-start.17
  198.9 1.5 copy-done.19
  200.5 1.6 pad_maximum_fusion
  202.2 13.5 %collective-permute-done.17.mine_ref = bf16[512,768]{1,0:T(8,128)(2,1)} collective-permute-done((bf16[512,768]{1,0:T(8,128)(2,1)S(1)}, bf16[512,768]{1,0:T(8,128)(2,1)}, u32[]{:S(2)}, u32[]{:S(2)}) %collective-permute-start.17) | collective-permute-done | bytes 786464 | tf_op jit(solution)/shard_map/ppermute | solution.py:715
  216.3 18.7 %shard_map.337 = (bf16[512,768]{1,0:T(8,128)(2,1)}, bf16[512,768]{1,0:T(8,128)(2,1)}, f32[768,768]{1,0:T(8,128)}, f32[8,256]{1,0:T(8,128)}) custom-call(s32[2]{0:T(128)} %get-tuple-element.174.where_ref, bf16[512,768]{1,0:T(8,128)(2,1)} %copy-done.23, bf16[512,768]{1,0:T(8,128)(2,1)} %collective-permute-done.15.theirs_ref, bf16[2,1024,768]{2,1,0:T(8,128)(2,1)} %bitcast.22, ...), custom_call_target="tpu_custom_call" | custom-call | flops 12000000000 | bytes 14000000 | tf_op jit(solution)/shard_map/pallas_call | solution.py:586
  235.9 18.8 %shard_map.338 = (bf16[512,768]{1,0:T(8,128)(2,1)}, bf16[512,768]{1,0:T(8,128)(2,1)}, f32[768,768]{1,0:T(8,128)}, f32[8,256]{1,0:T(8,128)}) custom-call(s32[2]{0:T(128)} %get-tuple-element.175.where_ref, bf16[512,768]{1,0:T(8,128)(2,1)} %collective-permute-done.17.mine_ref, bf16[512,768]{1,0:T(8,128)(2,1)} %copy-done.37, bf16[2,1024,768]{2,1,0:T(8,128)(2,1)} %bitcast.23, ...), custom_call_target="tpu_custom_call" | custom-call | flops 12000000000 | bytes 14000000 | tf_op jit(solution)/shard_map/pallas_call | solution.py:586
  255.3 2.8 convert_element_type.87
  258.1 53.3 %all-reduce.6.cloned.1.call-done = bf16[1536,768]{1,0:T(8,128)(2,1)} async-done(((bf16[1536,768]{1,0:T(8,128)(2,1)}), bf16[1536,768]{1,0:T(8,128)(2,1)}) %all-reduce.6.cloned.1.call-update) | async-done | bytes 2359312 | tf_op jit(solution)/shard_map/psum | solution.py:794
  311.7 1.2 collective-permute-done.21
  312.9 1.5 collective-permute-start.22
  315.1 1.6 collective-permute-done.22
  316.7 1.5 collective-permute-start.23
  318.3 2.6 collective-permute-done.23
  321.6 6.2 %collective-permute-done.24 = f32[12,768]{1,0:T(8,128)S(1)} collective-permute-done((f32[12,768]{1,0:T(8,128)S(1)}, f32[12,768]{1,0:T(8,128)S(1)}, u32[]{:S(2)}, u32[]{:S(2)}) %collective-permute-start.24) | collective-permute-done | bytes 36896 | tf_op jit(solution)/shard_map/ppermute | solution.py:715
  327.9 2.2 add.154
  330.1 1.4 collective-permute-start.20
  331.6 2.5 fusion.14
  334.1 1.8 collective-permute-done.25
  337.7 58.7 %all-reduce.8.cloned.1.call-done = bf16[768,768]{1,0:T(8,128)(2,1)} async-done(((bf16[768,768]{1,0:T(8,128)(2,1)}), bf16[768,768]{1,0:T(8,128)(2,1)}) %all-reduce.8.cloned.1.call-update) | async-done | bytes 1179664 | tf_op jit(solution)/shard_map/psum | solution.py:806
  396.5 1.5 convert_element_type.88
  399.0 1.2 slice_bitcast_fusion
  401.2 2.7 add_add_fusion
  (159 shorter events, 20.8 us)
Async XLA Ops:
  7.2 304.2 %all-reduce.6.cloned.1.call-start = ((), (), s32[]{:S(2)}) async-start(), calls=%async_computation | async-start | bytes 4718592 | tf_op jit(solution)/shard_map/psum | solution.py:794
  20.8 12.6 %collective-permute-start.1 = (bf16[512,768]{1,0:T(8,128)(2,1)}, bf16[512,768]{1,0:T(8,128)(2,1)S(1)}, u32[]{:S(2)}, u32[]{:S(2)}) collective-permute-start(bf16[512,768]{1,0:T(8,128)(2,1)} %get-tuple-element.83), channel_id=1, source_target_pairs={{0,1},{1,0},{2,3},{3,2},{4,5},{5,4},{6,7},{7,6},{8,9},{9,8},{10,11... | collective-permute-start | bytes 2359304 | tf_op jit(solution)/shard_map/ppermute | solution.py:715
  21.4 12.0 %copy-start.24 = (bf16[512,768]{1,0:T(8,128)(2,1)S(1)}, bf16[512,768]{1,0:T(8,128)(2,1)}, u32[]{:S(2)}) copy-start(bf16[512,768]{1,0:T(8,128)(2,1)} %get-tuple-element.82) | copy-start | bytes 2359300
  33.2 21.1 %copy-start.27 = (bf16[512,768]{1,0:T(8,128)(2,1)S(1)}, bf16[512,768]{1,0:T(8,128)(2,1)}, u32[]{:S(2)}) copy-start(bf16[512,768]{1,0:T(8,128)(2,1)} %get-tuple-element.80) | copy-start | bytes 2359300
  33.2 21.1 %copy-start.35 = (f32[768]{0:T(1024)S(1)}, f32[768]{0:T(1024)}, u32[]{:S(2)}) copy-start(f32[768]{0:T(1024)} %param.28) | copy-start | bytes 9220
  33.3 3.4 collective-permute-start
  33.6 20.8 %collective-permute-start.2 = (bf16[512,768]{1,0:T(8,128)(2,1)S(1)}, bf16[512,768]{1,0:T(8,128)(2,1)S(1)}, u32[]{:S(2)}, u32[]{:S(2)}) collective-permute-start(bf16[512,768]{1,0:T(8,128)(2,1)S(1)} %add.132), channel_id=1, source_target_pairs={{0,2},{1,3},{2,0},{3,1},{4,6},{5,7},{6,4},{7,5},{8,10},{9,11},{10,... | collective-permute-start | bytes 2359304 | tf_op jit(solution)/shard_map/ppermute | solution.py:715
  56.4 19.8 %copy-start.34 = (f32[768]{0:T(1024)S(1)}, f32[768]{0:T(1024)}, u32[]{:S(2)}) copy-start(f32[768]{0:T(1024)} %param.32) | copy-start | bytes 9220
  56.4 22.0 %copy-start.1 = (bf16[768,768]{1,0:T(8,128)(2,1)S(1)}, bf16[768,768]{1,0:T(8,128)(2,1)}, u32[]{:S(2)}) copy-start(bf16[768,768]{1,0:T(8,128)(2,1)} %refs_8_.3) | copy-start | bytes 3538948
  56.4 22.0 %copy-start.2 = (bf16[768,768]{1,0:T(8,128)(2,1)S(1)}, bf16[768,768]{1,0:T(8,128)(2,1)}, u32[]{:S(2)}) copy-start(bf16[768,768]{1,0:T(8,128)(2,1)} %refs_9_.3) | copy-start | bytes 3538948
  57.1 33.0 %copy-start = (bf16[512,768]{1,0:T(8,128)(2,1)}, bf16[512,768]{1,0:T(8,128)(2,1)S(1)}, u32[]{:S(2)}) copy-start(bf16[512,768]{1,0:T(8,128)(2,1)S(1)} %fusion.7.one_ref.refs_3_) | copy-start | bytes 2359300
  57.1 19.1 %collective-permute-start.5 = (bf16[512,768]{1,0:T(8,128)(2,1)S(1)}, bf16[512,768]{1,0:T(8,128)(2,1)S(1)}, u32[]{:S(2)}, u32[]{:S(2)}) collective-permute-start(bf16[512,768]{1,0:T(8,128)(2,1)S(1)} %fusion.7.one_ref.refs_3_), channel_id=1, source_target_pairs={{0,2},{1,3},{2,0},{3,1},{4,6},{5,7},{6,4},{7,5},{8,10},{9,11},{10,... | collective-permute-start | bytes 2359304 | tf_op jit(solution)/shard_map/ppermute | solution.py:715
  76.2 10.2 %copy-start.3 = (bf16[512,768]{1,0:T(8,128)(2,1)}, bf16[512,768]{1,0:T(8,128)(2,1)S(1)}, u32[]{:S(2)}) copy-start(bf16[512,768]{1,0:T(8,128)(2,1)S(1)} %collective-permute-done.5.one_ref.refs_3_) | copy-start | bytes 2359300
  76.2 2.3 collective-permute-start.6
  76.2 13.9 %collective-permute-start.3 = (bf16[512,768]{1,0:T(8,128)(2,1)S(1)}, bf16[512,768]{1,0:T(8,128)(2,1)S(1)}, u32[]{:S(2)}, u32[]{:S(2)}) collective-permute-start(bf16[512,768]{1,0:T(8,128)(2,1)S(1)} %fusion.7.one_ref.refs_3_), channel_id=1, source_target_pairs={{0,1},{1,0},{2,3},{3,2},{4,5},{5,4},{6,7},{7,6},{8,9},{9,8},{10,11... | collective-permute-start | bytes 2359304 | tf_op jit(solution)/shard_map/ppermute | solution.py:715
  90.0 8.1 %collective-permute-start.7 = (bf16[512,768]{1,0:T(8,128)(2,1)S(1)}, bf16[512,768]{1,0:T(8,128)(2,1)S(1)}, u32[]{:S(2)}, u32[]{:S(2)}) collective-permute-start(bf16[512,768]{1,0:T(8,128)(2,1)S(1)} %get-tuple-element.87), channel_id=1, source_target_pairs={{0,1},{1,0},{2,3},{3,2},{4,5},{5,4},{6,7},{7,6},{8,9},{9,8},{10,11... | collective-permute-start | bytes 2359304 | tf_op jit(solution)/shard_map/ppermute | solution.py:715
  97.6 21.2 %copy-start.10 = (bf16[512,768]{1,0:T(8,128)(2,1)}, bf16[512,768]{1,0:T(8,128)(2,1)S(1)}, u32[]{:S(2)}) copy-start(bf16[512,768]{1,0:T(8,128)(2,1)S(1)} %get-tuple-element.88.refs_1_) | copy-start | bytes 2359300
  97.6 21.2 %copy-start.11 = (bf16[512,768]{1,0:T(8,128)(2,1)}, bf16[512,768]{1,0:T(8,128)(2,1)S(1)}, u32[]{:S(2)}) copy-start(bf16[512,768]{1,0:T(8,128)(2,1)S(1)} %get-tuple-element.89.refs_2_) | copy-start | bytes 2359300
  97.6 21.2 %copy-start.12 = (bf16[512,768]{1,0:T(8,128)(2,1)}, bf16[512,768]{1,0:T(8,128)(2,1)S(1)}, u32[]{:S(2)}) copy-start(bf16[512,768]{1,0:T(8,128)(2,1)S(1)} %get-tuple-element.90.refs_5_) | copy-start | bytes 2359300
  97.7 21.2 %copy-start.13 = (bf16[512,768]{1,0:T(8,128)(2,1)}, bf16[512,768]{1,0:T(8,128)(2,1)S(1)}, u32[]{:S(2)}) copy-start(bf16[512,768]{1,0:T(8,128)(2,1)S(1)} %get-tuple-element.91.refs_6_) | copy-start | bytes 2359300
  97.7 20.3 %copy-start.33 = (f32[768]{0:T(1024)S(1)}, f32[768]{0:T(1024)}, u32[]{:S(2)}) copy-start(f32[768]{0:T(1024)} %param.34) | copy-start | bytes 9220
  97.7 2.4 collective-permute-start.4
  98.4 19.6 %collective-permute-start.8 = (bf16[512,768]{1,0:T(8,128)(2,1)S(1)}, bf16[512,768]{1,0:T(8,128)(2,1)S(1)}, u32[]{:S(2)}, u32[]{:S(2)}) collective-permute-start(bf16[512,768]{1,0:T(8,128)(2,1)S(1)} %add.141), channel_id=1, source_target_pairs={{0,2},{1,3},{2,0},{3,1},{4,6},{5,7},{6,4},{7,5},{8,10},{9,11},{10,... | collective-permute-start | bytes 2359304 | tf_op jit(solution)/shard_map/ppermute | solution.py:715
  122.6 21.1 %copy-start.25 = (bf16[512,768]{1,0:T(8,128)(2,1)}, bf16[512,768]{1,0:T(8,128)(2,1)S(1)}, u32[]{:S(2)}) copy-start(bf16[512,768]{1,0:T(8,128)(2,1)S(1)} %convert_element_type.79.refs_0_) | copy-start | bytes 2359300
  122.6 18.8 %collective-permute-start.11 = (bf16[512,768]{1,0:T(8,128)(2,1)S(1)}, bf16[512,768]{1,0:T(8,128)(2,1)S(1)}, u32[]{:S(2)}, u32[]{:S(2)}) collective-permute-start(bf16[512,768]{1,0:T(8,128)(2,1)S(1)} %convert_element_type.79.refs_0_), channel_id=1, source_target_pairs={{0,2},{1,3},{2,0},{3,1},{4,6},{5,7},{6,4},{7,5},{8,10},{9,11},{10,... | collective-permute-start | bytes 2359304 | tf_op jit(solution)/shard_map/ppermute | solution.py:715
  124.1 17.3 %collective-permute-start.9 = (bf16[512,768]{1,0:T(8,128)(2,1)S(1)}, bf16[512,768]{1,0:T(8,128)(2,1)S(1)}, u32[]{:S(2)}, u32[]{:S(2)}) collective-permute-start(bf16[512,768]{1,0:T(8,128)(2,1)S(1)} %convert_element_type.79.refs_0_), channel_id=1, source_target_pairs={{0,1},{1,0},{2,3},{3,2},{4,5},{5,4},{6,7},{7,6},{8,9},{9,8},{10,11... | collective-permute-start | bytes 2359304 | tf_op jit(solution)/shard_map/ppermute | solution.py:715
  141.3 14.9 %copy-start.39 = (bf16[512,768]{1,0:T(8,128)(2,1)}, bf16[512,768]{1,0:T(8,128)(2,1)S(1)}, u32[]{:S(2)}) copy-start(bf16[512,768]{1,0:T(8,128)(2,1)S(1)} %collective-permute-done.11.refs_0_) | copy-start | bytes 2359300
  141.4 14.9 %collective-permute-start.12 = (bf16[512,768]{1,0:T(8,128)(2,1)S(1)}, bf16[512,768]{1,0:T(8,128)(2,1)S(1)}, u32[]{:S(2)}, u32[]{:S(2)}) collective-permute-start(bf16[512,768]{1,0:T(8,128)(2,1)S(1)} %collective-permute-done.11.refs_0_), channel_id=1, source_target_pairs={{0,1},{1,0},{2,3},{3,2},{4,5},{5,4},{6,7},{7,6},{8,9},{9,8},{10,11... | collective-permute-start | bytes 2359304 | tf_op jit(solution)/shard_map/ppermute | solution.py:715
  157.1 12.9 %copy-start.38 = (bf16[512,768]{1,0:T(8,128)(2,1)S(1)}, bf16[512,768]{1,0:T(8,128)(2,1)}, u32[]{:S(2)}) copy-start(bf16[512,768]{1,0:T(8,128)(2,1)} %get-tuple-element.93) | copy-start | bytes 2359300
  169.5 24.1 %copy-start.21 = (bf16[512,768]{1,0:T(8,128)(2,1)S(1)}, bf16[512,768]{1,0:T(8,128)(2,1)}, u32[]{:S(2)}) copy-start(bf16[512,768]{1,0:T(8,128)(2,1)} %get-tuple-element.92) | copy-start | bytes 2359300
  169.5 2.9 collective-permute-start.13
  170.1 5.2 %collective-permute-start.10 = (bf16[512,768]{1,0:T(8,128)(2,1)S(1)}, bf16[512,768]{1,0:T(8,128)(2,1)S(1)}, u32[]{:S(2)}, u32[]{:S(2)}) collective-permute-start(bf16[512,768]{1,0:T(8,128)(2,1)S(1)} %copy-done.38), channel_id=1, source_target_pairs={{0,1},{1,0},{2,3},{3,2},{4,5},{5,4},{6,7},{7,6},{8,9},{9,8},{10,11... | collective-permute-start | bytes 2359304 | tf_op jit(solution)/shard_map/ppermute | solution.py:715
  173.8 19.9 %collective-permute-start.14 = (bf16[512,768]{1,0:T(8,128)(2,1)S(1)}, bf16[512,768]{1,0:T(8,128)(2,1)S(1)}, u32[]{:S(2)}, u32[]{:S(2)}) collective-permute-start(bf16[512,768]{1,0:T(8,128)(2,1)S(1)} %add.150), channel_id=1, source_target_pairs={{0,2},{1,3},{2,0},{3,1},{4,6},{5,7},{6,4},{7,5},{8,10},{9,11},{10,... | collective-permute-start | bytes 2359304 | tf_op jit(solution)/shard_map/ppermute | solution.py:715
  196.5 19.2 %collective-permute-start.17 = (bf16[512,768]{1,0:T(8,128)(2,1)S(1)}, bf16[512,768]{1,0:T(8,128)(2,1)}, u32[]{:S(2)}, u32[]{:S(2)}) collective-permute-start(bf16[512,768]{1,0:T(8,128)(2,1)S(1)} %convert_element_type.83.mine_ref), channel_id=1, source_target_pairs={{0,2},{1,3},{2,0},{3,1},{4,6},{5,7},{6,4},{7,5},{8,10},{9,11},{10,... | collective-permute-start | bytes 2359304 | tf_op jit(solution)/shard_map/ppermute | solution.py:715
  198.0 17.7 %collective-permute-start.15 = (bf16[512,768]{1,0:T(8,128)(2,1)S(1)}, bf16[512,768]{1,0:T(8,128)(2,1)}, u32[]{:S(2)}, u32[]{:S(2)}) collective-permute-start(bf16[512,768]{1,0:T(8,128)(2,1)S(1)} %convert_element_type.83.mine_ref), channel_id=1, source_target_pairs={{0,1},{1,0},{2,3},{3,2},{4,5},{5,4},{6,7},{7,6},{8,9},{9,8},{10,11... | collective-permute-start | bytes 2359304 | tf_op jit(solution)/shard_map/ppermute | solution.py:715
  202.1 194.4 %all-reduce.8.cloned.1.call-start = ((), (), s32[]{:S(2)}) async-start(), calls=%async_computation.1 | async-start | bytes 2359296 | tf_op jit(solution)/shard_map/psum | solution.py:806
  215.7 19.3 %collective-permute-start.18 = (bf16[512,768]{1,0:T(8,128)(2,1)}, bf16[512,768]{1,0:T(8,128)(2,1)S(1)}, u32[]{:S(2)}, u32[]{:S(2)}) collective-permute-start(bf16[512,768]{1,0:T(8,128)(2,1)} %collective-permute-done.17.mine_ref), channel_id=1, source_target_pairs={{0,1},{1,0},{2,3},{3,2},{4,5},{5,4},{6,7},{7,6},{8,9},{9,8},{10,11... | collective-permute-start | bytes 2359304 | tf_op jit(solution)/shard_map/ppermute | solution.py:715
  254.7 73.2 %collective-permute-start.19 = (bf16[512,768]{1,0:T(8,128)(2,1)}, bf16[512,768]{1,0:T(8,128)(2,1)}, u32[]{:S(2)}, u32[]{:S(2)}) collective-permute-start(bf16[512,768]{1,0:T(8,128)(2,1)} %get-tuple-element.134), channel_id=1, source_target_pairs={{0,1},{1,0},{2,3},{3,2},{4,5},{5,4},{6,7},{7,6},{8,9},{9,8},{10,11... | collective-permute-start | bytes 2359304 | tf_op jit(solution)/shard_map/ppermute | solution.py:715
  255.3 61.4 %copy-start.29 = (f32[8,256]{1,0:T(8,128)S(1)}, f32[8,256]{1,0:T(8,128)}, u32[]{:S(2)}) copy-start(f32[8,256]{1,0:T(8,128)} %get-tuple-element.140) | copy-start | bytes 24580
  258.1 69.8 %copy-start.22 = (bf16[512,768]{1,0:T(8,128)(2,1)S(1)}, bf16[512,768]{1,0:T(8,128)(2,1)}, u32[]{:S(2)}) copy-start(bf16[512,768]{1,0:T(8,128)(2,1)} %get-tuple-element.133) | copy-start | bytes 2359300
  311.5 20.1 %copy-start.16 = (bf16[1536,768]{1,0:T(8,128)(2,1)S(1)}, bf16[1536,768]{1,0:T(8,128)(2,1)}, u32[]{:S(2)}) copy-start(bf16[1536,768]{1,0:T(8,128)(2,1)} %all-reduce.6.cloned.1.call-done) | copy-start | bytes 7077892
  311.6 1.3 collective-permute-start.21
  312.9 3.8 collective-permute-start.22
  316.7 4.2 %collective-permute-start.23 = (f32[12,768]{1,0:T(8,128)S(1)}, f32[12,768]{1,0:T(8,128)S(1)}, u32[]{:S(2)}, u32[]{:S(2)}) collective-permute-start(f32[12,768]{1,0:T(8,128)S(1)} %select_maximum_fusion), channel_id=1, source_target_pairs={{0,4},{4,0},{8,12},{12,8},{16,20},{20,16},{24,28},{28,24},{1,5},{5... | collective-permute-start | bytes 110600 | tf_op jit(solution)/shard_map/ppermute | solution.py:715
  320.9 6.9 %collective-permute-start.24 = (f32[12,768]{1,0:T(8,128)S(1)}, f32[12,768]{1,0:T(8,128)S(1)}, u32[]{:S(2)}, u32[]{:S(2)}) collective-permute-start(f32[12,768]{1,0:T(8,128)S(1)} %fusion.8), channel_id=1, source_target_pairs={{0,8},{4,12},{8,0},{12,4},{16,24},{20,28},{24,16},{28,20},{1,9},{5... | collective-permute-start | bytes 110600 | tf_op jit(solution)/shard_map/ppermute | solution.py:715
  321.6 78.6 %collective-permute-start.16 = (bf16[512,768]{1,0:T(8,128)(2,1)}, bf16[512,768]{1,0:T(8,128)(2,1)}, u32[]{:S(2)}, u32[]{:S(2)}) collective-permute-start(bf16[512,768]{1,0:T(8,128)(2,1)} %get-tuple-element.117), channel_id=1, source_target_pairs={{0,1},{1,0},{2,3},{3,2},{4,5},{5,4},{6,7},{7,6},{8,9},{9,8},{10,11... | collective-permute-start | bytes 2359304 | tf_op jit(solution)/shard_map/ppermute | solution.py:715
  327.8 8.1 %collective-permute-start.25 = (f32[12,768]{1,0:T(8,128)S(1)}, f32[12,768]{1,0:T(8,128)S(1)}, u32[]{:S(2)}, u32[]{:S(2)}) collective-permute-start(f32[12,768]{1,0:T(8,128)S(1)} %add.160), channel_id=1, source_target_pairs={{0,16},{4,20},{8,24},{12,28},{16,0},{20,4},{24,8},{28,12},{1,17},{... | collective-permute-start | bytes 110600 | tf_op jit(solution)/shard_map/ppermute | solution.py:715
  330.1 70.1 %collective-permute-start.20 = (bf16[512,768]{1,0:T(8,128)(2,1)}, bf16[512,768]{1,0:T(8,128)(2,1)S(1)}, u32[]{:S(2)}, u32[]{:S(2)}) collective-permute-start(bf16[512,768]{1,0:T(8,128)(2,1)} %add.154), channel_id=1, source_target_pairs={{0,2},{1,3},{2,0},{3,1},{4,6},{5,7},{6,4},{7,5},{8,10},{9,11},{10,... | collective-permute-start | bytes 2359304 | tf_op jit(solution)/shard_map/ppermute | solution.py:715
  (22 other events, 46.2 us)
Sparse Core Ops, SparseCore 0:
  202.2 109.1 all-reduce.5
  315.3 81.1 all-reduce.7
